TPU v7x, 128 devices: a whole 4x4x4 slice. The times are simulated.
128 devices in a mesh: rows: 32 (over x, z, core), feat: 4 (over y).
Axes of the slice: x: 4, y: 4, z: 4, core: 2. Of those that a mesh axis runs over, the one named last changes fastest.
Arguments:
- binned: int32 [65536, 256], P('rows', 'feat'), may hold values from 0 to 255
- node_index: int32 [65536, 1], P('rows'), may hold values from 0 to 31; in each aligned block of 2048 rows (0 to 2047, 2048 to 4095, ...) at most 128 rows name the same one
- treatment: float32 [65536], P('rows'), may hold values from -6 to 6
- outcome: float32 [65536], P('rows'), may hold values from -6 to 6
- unit_weight: float32 [65536], P('rows'), may hold values from 0.1 to 2
- root_feature: int32 [32], replicated, may hold values from 0 to 255
- root_cutoff: int32 [32], replicated, may hold values from 64 to 191
- child_feature: int32 [64], replicated, may hold values from 0 to 255
- child_cutoff: int32 [64], replicated, may hold values from 64 to 191
Outputs:
- node_moments: float32 [32, 3, 256, 256], P('rows', None, 'feat')
- child_moments: float32 [64, 3, 256, 256], P('rows', None, 'feat')
- leaf_moments: float32 [128, 3, 256, 256], P('rows', None, 'feat')
Inputs may be any that keep to these rules, and one draw needn't show every extreme that they name: `node_index`: among the rows of one device no node is named by more than 128 rows, a bound that some block reaches.
All inputs are finite; a program needn't handle non-finite values.
Results may differ from a plain program's by a relative error of at most 0.0022.
Values may be sent and summed in bfloat16 or wider, within the bound.
No kernel may reach another device: no remote copies, remote signals or barrier semaphores. Data moves between devices by JAX's collectives and lax.ppermute only.
A program may use at most 64 MiB of HBM per device.

v0:
```python
import jax
import jax.numpy as jnp
from jax import lax
from jax.sharding import PartitionSpec as P

BINS = 256


def histogram(weighted, features):
    feat_count, unit_count = features.shape
    blocks = features.reshape(feat_count // 4, 4, unit_count)
    levels = jnp.arange(BINS).astype(features.dtype)

    def one_block(carry, block):
        table = (block[:, :, None] == levels).astype(jnp.bfloat16)
        part = jnp.einsum("sc,fsb->cfb", weighted, table, preferred_element_type=jnp.float32)
        return (carry, part)

    unused, parts = lax.scan(one_block, 0, blocks)
    return jnp.moveaxis(parts, 0, 1).reshape(weighted.shape[1], feat_count, BINS)


def weigh(groups, group_count, moments):
    chosen = groups[:, None] == jnp.arange(group_count)
    spread = jnp.where(chosen[:, :, None], moments[:, None, :], jnp.zeros((), jnp.bfloat16))
    return spread.reshape(moments.shape[0], group_count * 3)


def on_device(
    binned,
    node_index,
    treatment,
    outcome,
    unit_weight,
    root_feature,
    root_cutoff,
    child_feature,
    child_cutoff,
):
    rows_here, feat_here = binned.shape
    node_count = root_feature.shape[0]
    owners = lax.axis_size("rows")
    per_owner = node_count // owners
    capacity = 2 * rows_here // node_count
    tree_node = node_index[:, 0]
    moments = jnp.stack(
        [unit_weight, unit_weight * treatment * treatment, unit_weight * treatment * outcome], 1
    ).astype(jnp.bfloat16)
    feature_major = binned.T
    first_child = 2 * tree_node
    wanted = jnp.stack(
        [root_feature[tree_node], child_feature[first_child], child_feature[first_child + 1]], 0
    )
    wanted = wanted - lax.axis_index("feat") * feat_here
    local_index = jnp.arange(feat_here)
    picked = jnp.sum(jnp.where(wanted[:, :, None] == local_index, binned[None, :, :], 0), axis=2)
    split_values = lax.psum(picked.astype(jnp.float32), "feat").astype(jnp.int32)
    right_root = (split_values[0] > root_cutoff[tree_node]).astype(jnp.int32)
    right_child = jnp.where(
        right_root == 1,
        split_values[2] > child_cutoff[first_child + 1],
        split_values[1] > child_cutoff[first_child],
    ).astype(jnp.int32)
    leaf_code = 2 * right_root + right_child
    all_weighted = weigh(tree_node, node_count, moments)
    all_terms = histogram(all_weighted, feature_major).reshape(node_count, 3, feat_here, BINS)
    node_moments = lax.psum_scatter(all_terms, "rows", scatter_dimension=0, tiled=True)
    node_onehot = (tree_node[:, None] == jnp.arange(node_count)).astype(jnp.int32)
    rank_in_node = jnp.sum(jnp.cumsum(node_onehot, 0) * node_onehot, 1) - 1
    slot_index = tree_node * capacity + rank_in_node
    feat_buffer = (
        jnp.zeros((feat_here, node_count * capacity), jnp.bfloat16)
        .at[:, slot_index]
        .set(feature_major.astype(jnp.bfloat16))
    )
    carried = jnp.concatenate([moments.T, leaf_code[None, :].astype(jnp.bfloat16)], 0)
    moment_buffer = (
        jnp.zeros((4, node_count * capacity), jnp.bfloat16).at[:, slot_index].set(carried)
    )
    feat_buffer = feat_buffer.reshape(feat_here, owners, per_owner * capacity)
    moment_buffer = moment_buffer.reshape(4, owners, per_owner * capacity)
    got_feat, got_moment = (
        lax.all_to_all(feat_buffer, "rows", split_axis=1, concat_axis=1, tiled=True),
        lax.all_to_all(moment_buffer, "rows", split_axis=1, concat_axis=1, tiled=True),
    )
    slots = owners * per_owner * capacity
    got_feat = got_feat.reshape(feat_here, slots)
    got_moment = got_moment.reshape(4, slots)
    owned_node = jnp.arange(slots) % (per_owner * capacity) // capacity
    got_leaf = got_moment[3].astype(jnp.int32)
    got_values = got_moment[:3].T
    leaf_weighted = weigh(4 * owned_node + got_leaf, 4 * per_owner, got_values)
    leaf_moments = histogram(leaf_weighted, got_feat).reshape(4 * per_owner, 3, feat_here, BINS)
    child_moments = leaf_moments.reshape(2 * per_owner, 2, 3, feat_here, BINS).sum(1)
    return (node_moments, child_moments, leaf_moments)


def solution(mesh):
    in_specs = (
        P("rows", "feat"),
        P("rows", None),
        P("rows"),
        P("rows"),
        P("rows"),
        P(),
        P(),
        P(),
        P(),
    )
    out_specs = (
        P("rows", None, "feat", None),
        P("rows", None, "feat", None),
        P("rows", None, "feat", None),
    )
    return jax.shard_map(
        on_device, mesh=mesh, in_specs=in_specs, out_specs=out_specs, check_vma=False
    )
```

profile of v0, /device:TPU:1, one launch (start us, length us, event | category | flops | bytes accessed | tf_op | source)
XLA Modules:
  0.0 438.4 jit_solution(8207467654154019221)
XLA Ops:
  7.2 1.2 reshape.194
  8.4 0.8 multiply_convert_fusion.1
  9.2 0.7 iota_compare_fusion.8
  10.0 59.8 %while.22 = (s32[]{:T(128)}, f32[16,96,4,256]{3,1,2,0:T(8,128)}, s32[16,4,2048]{2,1,0:T(4,128)S(1)}, bf16[2048,3]{0,1:T(4,128)(2,1)S(1)}, pred[2048,32]{0,1:T(8,128)(4,1)S(1)}, /*index=5*/s32[]{:T(128)}) while((s32[]{:T(128)}, f32[16,96,4,256]{3,1,2,0:T(8,128)}, s32[16,4,2048]{2,1,0:T(4,128)S(1)}, bf16[2048,3]{0,1:T(4,128)(2,1)S(1)}, ...), condition=%wide.region_1.2_spmd.clone, body=%wide.region_0.1_spmd.clone.sunk | while | flops 404946944 | bytes 2142293 | solution.py:19
  10.8 3.0 fusion.58
  14.6 2.9 fusion.58
  18.3 2.9 fusion.58
  22.0 3.0 fusion.58
  25.7 2.9 fusion.58
  29.5 3.0 fusion.58
  33.2 3.0 fusion.58
  36.9 3.0 fusion.58
  40.7 3.0 fusion.58
  44.4 2.9 fusion.58
  48.2 3.0 fusion.58
  51.9 3.0 fusion.58
  55.6 3.0 fusion.58
  59.4 3.0 fusion.58
  63.1 3.0 fusion.58
  66.9 3.0 fusion.58
  69.8 9.5 %copy.52 = f32[96,16,4,256]{3,2,1,0:T(4,128)} copy(f32[96,16,4,256]{3,0,2,1:T(8,128)} %bitcast.279) | data formatting | bytes 12582912 | tf_op jit(solution)/shard_map/transpose | solution.py:20
  79.3 7.7 %reshape_reshape.9 = f32[32,3,64,256]{3,2,1,0:T(8,128)} reshape(f32[96,16,4,256]{3,2,1,0:T(4,128)} %copy.52) | data formatting | bytes 12582912 | tf_op jit(solution)/shard_map/reshape;reshape | solution.py:66
  89.0 0.7 fusion.47
  91.2 9.2 %reduce-window.6 = s32[32,16,128]{2,1,0:T(8,128)S(1)} reduce-window(s32[32,16,128]{2,1,0:T(8,128)S(1)} %fusion.28, s32[]{:T(128)} %copy.84), window={size=1x1x128 pad=0_0x0_0x127_0}, to_apply=%region_3.4 | reduce-window | flops 8323072 | bytes 524292 | tf_op jit(solution)/shard_map/reduce-window
  101.3 4.6 %compare_select_fusion.5 = (s32[2048,1]{0,1:T(1,128)S(1)}, s32[2048,1]{0,1:T(1,128)S(1)}) fusion(s32[]{:T(128)} %bitcast.205, s32[]{:T(128)} %bitcast.206, s32[]{:T(128)} %bitcast.207, s32[]{:T(128)} %bitcast.208, s32[]{:T(128)} %bitcast.209, s32[]{:T(128)} %bitcast.211, s32[]{:T(128)} %bitcast.210, s32[2048,1]{0,1:T(1,128)S(1)} %copy-done.5), kind=kLoop, calls=%fused_computation.189 | loop fusion | flops 34816 | bytes 24604 | tf_op jit(solution)/shard_map/gather | solution.py:61
  105.9 8.8 %compare_select_fusion.29 = (s32[2048,1]{0,1:T(1,128)S(1)}, s32[2048,1]{0,1:T(1,128)S(1)}, s32[2048,1]{0,1:T(1,128)S(1)}, s32[2048,1]{0,1:T(1,128)S(1)}, s32[2048,1]{0,1:T(1,128)S(1)}, /*index=5*/s32[2048,1]{0,1:T(1,128)S(1)}) fusion(s32[]{:T(128)} %bitcast.139, s32[]{:T(128)} %bitcast.140, s32[]{:T(128)} %bitcast.141, s32[]{:T(128)} %bitcast.142, ...), kind=kLoop, calls=%fused_computation.213 | loop fusion | flops 98304 | bytes 73784 | tf_op jit(solution)/shard_map/gather | solution.py:58
  114.7 1.4 compare_reduce_fusion.113
  116.1 4.6 %compare_select_fusion.17 = s32[2048,1]{0,1:T(1,128)S(1)} fusion(s32[2048,1]{0,1:T(1,128)S(1)} %get-tuple-element.257, s32[]{:T(128)} %bitcast.205, s32[]{:T(128)} %bitcast.206, s32[]{:T(128)} %bitcast.207, s32[]{:T(128)} %bitcast.208, s32[]{:T(128)} %bitcast.209, s32[]{:T(128)} %bitcast.211, s32[]{:T(128)} %bitcast.210), kind=kLoop, calls=%fused_computation.201 | loop fusion | flops 24576 | bytes 16412 | tf_op jit(solution)/shard_map/gather | solution.py:62
  122.2 1.4 compare_reduce_fusion.56
  125.8 0.7 fusion.39
  127.9 4.2 compare_select_fusion.28
  132.1 15.5 %select_select_fusion.5 = s32[2048]{0:T(1024)S(1)} fusion(pred[2048]{0:T(1024)(128)(4,1)S(1)} %get-tuple-element.113, pred[2048]{0:T(1024)(128)(4,1)S(1)} %get-tuple-element.112, pred[2048]{0:T(1024)(128)(4,1)S(1)} %get-tuple-element.111, pred[2048]{0:T(1024)(128)(4,1)S(1)} %get-tuple-element.110, pred[2048]{0:T(1024)(128)(4,1)S(1)} %get-tuple-element.109, ...), kind=kLoop, calls=%fused_computation.243 | loop fusion | flops 51200 | bytes 67684 | tf_op jit(solution)/shard_map/gather | solution.py:52
  147.7 35.8 %select_select_fusion.3 = s32[2048]{0:T(1024)S(1)} fusion(pred[2048]{0:T(1024)(128)(4,1)S(1)} %get-tuple-element.170, pred[2048]{0:T(1024)(128)(4,1)S(1)} %get-tuple-element.169, pred[2048]{0:T(1024)(128)(4,1)S(1)} %get-tuple-element.168, pred[2048]{0:T(1024)(128)(4,1)S(1)} %get-tuple-element.167, pred[2048]{0:T(1024)(128)(4,1)S(1)} %get-tuple-element.166, ...), kind=kLoop, calls=%fused_computation.241 | loop fusion | flops 116736 | bytes 133348 | tf_op jit(solution)/shard_map/gather | solution.py:52
  183.5 35.8 %select_select_fusion.4 = s32[2048]{0:T(1024)S(1)} fusion(pred[2048]{0:T(1024)(128)(4,1)S(1)} %get-tuple-element.227, pred[2048]{0:T(1024)(128)(4,1)S(1)} %get-tuple-element.226, pred[2048]{0:T(1024)(128)(4,1)S(1)} %get-tuple-element.225, pred[2048]{0:T(1024)(128)(4,1)S(1)} %get-tuple-element.224, pred[2048]{0:T(1024)(128)(4,1)S(1)} %get-tuple-element.223, ...), kind=kLoop, calls=%fused_computation.242 | loop fusion | flops 116736 | bytes 133348 | tf_op jit(solution)/shard_map/gather | solution.py:52
  219.6 14.4 %psum.7 = f32[3,2048]{1,0:T(4,128)S(1)} all-reduce(f32[3,2048]{1,0:T(4,128)S(1)} %convert_element_type.50), channel_id=1, replica_groups=mesh['rows'=32,'feat'=4] {'feat'}, use_global_device_ids=true, to_apply=%region_8.9 | all-reduce | flops 6144 | bytes 49152 | tf_op jit(solution)/shard_map/psum | solution.py:57
  234.0 35.7 %select_select_fusion = s32[2048]{0:T(1024)S(1)} fusion(pred[2048]{0:T(1024)(128)(4,1)S(1)} %get-tuple-element.227, pred[2048]{0:T(1024)(128)(4,1)S(1)} %get-tuple-element.226, pred[2048]{0:T(1024)(128)(4,1)S(1)} %get-tuple-element.225, pred[2048]{0:T(1024)(128)(4,1)S(1)} %get-tuple-element.224, pred[2048]{0:T(1024)(128)(4,1)S(1)} %get-tuple-element.223, ...), kind=kLoop, calls=%fused_computation.238 | loop fusion | flops 116736 | bytes 133348 | tf_op jit(solution)/shard_map/gather | solution.py:62
  269.8 35.7 %select_select_fusion.1 = s32[2048]{0:T(1024)S(1)} fusion(pred[2048]{0:T(1024)(128)(4,1)S(1)} %get-tuple-element.170, pred[2048]{0:T(1024)(128)(4,1)S(1)} %get-tuple-element.169, pred[2048]{0:T(1024)(128)(4,1)S(1)} %get-tuple-element.168, pred[2048]{0:T(1024)(128)(4,1)S(1)} %get-tuple-element.167, pred[2048]{0:T(1024)(128)(4,1)S(1)} %get-tuple-element.166, ...), kind=kLoop, calls=%fused_computation.239 | loop fusion | flops 116736 | bytes 133348 | tf_op jit(solution)/shard_map/gather | solution.py:61
  305.5 15.7 %select_select_fusion.2 = s32[2048]{0:T(1024)S(1)} fusion(pred[2048]{0:T(1024)(128)(4,1)S(1)} %get-tuple-element.113, pred[2048]{0:T(1024)(128)(4,1)S(1)} %get-tuple-element.112, pred[2048]{0:T(1024)(128)(4,1)S(1)} %get-tuple-element.111, pred[2048]{0:T(1024)(128)(4,1)S(1)} %get-tuple-element.110, pred[2048]{0:T(1024)(128)(4,1)S(1)} %get-tuple-element.109, ...), kind=kLoop, calls=%fused_computation.240 | loop fusion | flops 51200 | bytes 67684 | tf_op jit(solution)/shard_map/gather | solution.py:58
  321.6 6.1 %scatter_custom_fusion.1 = bf16[4,4096]{0,1:T(8,128)(2,1)S(1)} fusion(s32[2048]{0:T(1024)S(1)} %bitcast.303, bf16[2048,4]{1,0:T(8,128)(2,1)S(1)} %copy.58, bf16[]{:T(256)} %constant.69.clone.1), kind=kCustom, calls=%fused_computation.24 | custom fusion | bytes 32770 | tf_op jit(solution)/shard_map/scatter | solution.py:78
  327.7 1.0 copy.59
  328.7 12.3 %all-to-all-start.1 = ((bf16[4,32,128]{2,0,1:T(4,128)(2,1)}), bf16[4,32,128]{2,0,1:T(4,128)(2,1)S(1)}, u32[]{:S(2)}, u32[]{:S(2)}) async-start(bf16[4,32,128]{2,0,1:T(4,128)(2,1)} %copy.59), calls=%async_computation.2 | async-start | bytes 65536 | tf_op jit(solution)/shard_map/all_to_all | solution.py:84
  341.4 6.1 %scatter_custom_fusion = bf16[64,4096]{0,1:T(8,128)(2,1)S(1)} fusion(s32[2048]{0:T(1024)S(1)} %bitcast.304, bf16[2048,64]{1,0:T(8,128)(2,1)S(1)} %copy.55, bf16[]{:T(256)} %constant.69.clone.1), kind=kCustom, calls=%fused_computation.26 | custom fusion | bytes 524290 | tf_op jit(solution)/shard_map/scatter | solution.py:74
  347.4 1.1 copy.56
  348.6 7.4 %all-to-all-start = ((bf16[64,32,128]{2,0,1:T(8,128)(2,1)}), bf16[64,32,128]{2,0,1:T(8,128)(2,1)S(1)}, u32[]{:S(2)}, u32[]{:S(2)}) async-start(bf16[64,32,128]{2,0,1:T(8,128)(2,1)} %copy.56), calls=%async_computation.1 | async-start | bytes 1048576 | tf_op jit(solution)/shard_map/all_to_all | solution.py:83
  356.1 11.5 %all-to-all-done = bf16[64,32,128]{2,0,1:T(8,128)(2,1)S(1)} async-done(((bf16[64,32,128]{2,0,1:T(8,128)(2,1)}), bf16[64,32,128]{2,0,1:T(8,128)(2,1)S(1)}, u32[]{:S(2)}, u32[]{:S(2)}) %all-to-all-start) | async-done | bytes 524320 | tf_op jit(solution)/shard_map/all_to_all | solution.py:83
  368.1 60.7 %while.23 = (s32[]{:T(128)}, f32[16,12,4,256]{3,1,2,0:T(8,128)S(1)}, bf16[16,4,4096]{2,1,0:T(4,128)(2,1)S(1)}, bf16[4096,3]{0,1:T(4,128)(2,1)S(1)}, pred[4096,4]{0,1:T(4,128)(4,1)S(1)}, /*index=5*/s32[]{:T(128)}) while((s32[]{:T(128)}, f32[16,12,4,256]{3,1,2,0:T(8,128)S(1)}, bf16[16,4,4096]{2,1,0:T(4,128)(2,1)S(1)}, ...), condition=%wide.region_11.12_spmd.clone, body=%wide.region_10.11_spmd.clone.sunk | while | flops 104907008 | bytes 631893 | solution.py:19
  368.3 3.5 fusion.61
  372.1 3.5 fusion.61
  375.9 3.5 fusion.61
  379.7 3.5 fusion.61
  383.5 3.5 fusion.61
  387.3 3.5 fusion.61
  391.1 3.5 fusion.61
  394.9 3.5 fusion.61
  398.7 3.5 fusion.61
  402.5 3.5 fusion.61
  406.3 3.5 fusion.61
  410.1 3.5 fusion.61
  413.8 3.5 fusion.61
  417.6 3.5 fusion.61
  421.4 3.5 fusion.61
  425.2 3.5 fusion.61
  429.6 1.1 reshape_reshape.11
  430.7 0.8 reduce_sum.29
  (170 shorter events, 27.6 us)
Async XLA Ops:
  7.2 424.4 %reduce-scatter.2.cloned.1.call-start = ((), (), s32[]{:S(2)}) async-start(), calls=%async_computation.3 | async-start | bytes 6488064 | tf_op jit(solution)/shard_map/reduce_scatter | solution.py:67
  87.0 0.7 copy-start.2
  87.0 2.1 copy-start.1
  87.0 3.5 copy-start.4
  87.0 4.2 copy-start.5
  87.0 38.1 %copy-start.3 = (s32[32]{0:T(128)S(1)}, s32[32]{0:T(128)}, u32[]{:S(2)}) copy-start(s32[32]{0:T(128)} %param.18) | copy-start | bytes 388
  87.0 132.4 %copy-start = (s32[2048,64]{0,1:T(8,128)S(1)}, s32[2048,64]{0,1:T(8,128)}, u32[]{:S(2)}) copy-start(s32[2048,64]{0,1:T(8,128)} %param.13) | copy-start | bytes 1572868
  328.7 19.9 %all-to-all-start.1 = ((bf16[4,32,128]{2,0,1:T(4,128)(2,1)}), bf16[4,32,128]{2,0,1:T(4,128)(2,1)S(1)}, u32[]{:S(2)}, u32[]{:S(2)}) async-start(bf16[4,32,128]{2,0,1:T(4,128)(2,1)} %copy.59), calls=%async_computation.2 | async-start | bytes 65536 | tf_op jit(solution)/shard_map/all_to_all | solution.py:84
  348.6 19.0 %all-to-all-start = ((bf16[64,32,128]{2,0,1:T(8,128)(2,1)}), bf16[64,32,128]{2,0,1:T(8,128)(2,1)S(1)}, u32[]{:S(2)}, u32[]{:S(2)}) async-start(bf16[64,32,128]{2,0,1:T(8,128)(2,1)} %copy.56), calls=%async_computation.1 | async-start | bytes 1048576 | tf_op jit(solution)/shard_map/all_to_all | solution.py:83
Sparse Core Ops, SparseCore 0:
  87.2 88.0 reduce-scatter.1
where the time goes:
time: 442 us; the launch traced here: 438 us
  other arithmetic  221 us (50%)
  matrix products  104 us (24%)
  local copies, waits for them, and re-layouts  52.5 us (12%)
  starting transfers between devices  19.8 us (4%)
  blocking collectives  14.4 us (3%)
  between operations  14.4 us (3%)
  waiting for transfers between devices  11.5 us (3%)
    dot_general x32, matrix products, one_block(): jnp.einsum('sc,fsb->cfb', weighted, table, preferred_element_type=jnp.flo...  104 us
    gather x2, other arithmetic, on_device(): child_cutoff[first_child + 1]  40.3 us
    gather x2, other arithmetic, on_device(): child_cutoff[first_child]  40.3 us
    gather x2, other arithmetic, on_device(): child_feature[first_child]  37.3 us
    gather x2, other arithmetic, on_device(): child_feature[first_child + 1]  37.3 us
    gather x2, other arithmetic, on_device(): right_root = (split_values[0] > root_cutoff[tree_node]).astype(jnp.int32)  24.5 us
    gather x3, other arithmetic, on_device(): root_feature[tree_node]  20.4 us
    psum x1, blocking collectives, on_device(): lax.psum(picked.astype(jnp.float32), 'feat').astype(jnp.int32)  14.4 us
  transfers between devices with their start and end apart: 3, of which 1 were waited for; matrix products, arithmetic and copies ran while one was open for 68% of the time, Pallas kernels for 0%

commit v1 on v0

v1 whole, which is shorter than its diff:
```python
import jax
import jax.numpy as jnp
from jax import lax
from jax.experimental import pallas as pl
from jax.experimental.pallas import tpu as pltpu
from jax.sharding import PartitionSpec as P

BINS = 256
BF = jnp.bfloat16
F32 = jnp.float32
NT = (((1,), (1,)), ((), ()))
NN = (((1,), (0,)), ((), ()))


def iota(shape, axis):
    return lax.broadcasted_iota(jnp.int32, shape, axis)


def split_kernel(where_ref, bins_ref, node_ref, rf_ref, rc_ref, cf_ref, cc_ref, bits_ref):
    feats, rows = bins_ref.shape
    nodes = rf_ref.shape[1]
    first = where_ref[0] * feats
    bins = bins_ref[...].astype(F32)
    node = node_ref[...]

    def decide(feature_row, cutoff_row, index, count):
        here = (feature_row - first == iota((feats, count), 0)).astype(F32)
        table = jnp.concatenate([here, jnp.broadcast_to(cutoff_row.astype(F32), (8, count))], 0)
        hot = (iota((count, rows), 0) == index).astype(F32).astype(BF)
        got = lax.dot_general(table.astype(BF), hot, NN, preferred_element_type=F32)
        right = jnp.where(bins > got[feats : feats + 1], got[:feats], 0.0)
        return jnp.sum(right, 0, keepdims=True)

    root = decide(rf_ref[...], rc_ref[...], node, nodes)
    left = decide(cf_ref[...], cc_ref[...], 2 * node, 2 * nodes)
    right = decide(cf_ref[...], cc_ref[...], 2 * node + 1, 2 * nodes)
    bits_ref[...] = jnp.concatenate([root, left, right, jnp.zeros((5, rows), F32)], 0).astype(BF)


def place_kernel(bins_ref, node_ref, out_ref, code_ref, a_ref):
    feats, rows = bins_ref.shape
    nodes, _, cap = out_ref.shape
    blocks = rows // 256
    node = node_ref[...]
    hot = (iota((nodes, rows), 0) == node).astype(F32)
    stacked = jnp.concatenate([hot[:, b * 256 : (b + 1) * 256] for b in range(blocks)], 0)
    before = (iota((256, 256), 0) < iota((256, 256), 1)).astype(F32).astype(BF)
    ones = jnp.ones((256, 256), BF)
    inner = lax.dot_general(stacked.astype(BF), before, NN, preferred_element_type=F32)
    total = lax.dot_general(stacked.astype(BF), ones, NN, preferred_element_type=F32)
    carry = jnp.zeros((nodes, 256), F32)
    ranks = []
    for b in range(blocks):
        part = slice(b * nodes, (b + 1) * nodes)
        ranks.append(jnp.sum(stacked[part] * (inner[part] + carry), 0, keepdims=True))
        carry = carry + total[part]
    rank = jnp.concatenate(ranks, 1)
    code = rank + (node % 2 * cap).astype(F32)
    code_ref[...] = code
    slot_hot = (iota((2 * cap, rows), 0) == code.astype(jnp.int32)).astype(F32).astype(BF)
    bins = bins_ref[...].astype(F32).astype(BF)
    pair = jnp.broadcast_to(node // 2, (feats, rows))
    for p in range(nodes // 2):
        a_ref[p * feats : (p + 1) * feats, :] = jnp.where(pair == p, bins, jnp.zeros((), BF))
    moved = lax.dot_general(a_ref[...], slot_hot, NT, preferred_element_type=F32).astype(BF)
    for p in range(nodes // 2):
        piece = moved[p * feats : (p + 1) * feats]
        out_ref[2 * p, :feats, :] = piece[:, :cap]
        out_ref[2 * p + 1, :feats, :] = piece[:, cap:]


def value_kernel(
    b0_ref, b1_ref, b2_ref, b3_ref, node_ref, code_ref, w_ref, t_ref, y_ref, buf_ref, out_ref,
    part_ref, sem,
):
    nodes, _, cap = part_ref.shape
    rows = node_ref.shape[1]
    bits = (b0_ref[...].astype(F32) + b1_ref[...].astype(F32)) + (
        b2_ref[...].astype(F32) + b3_ref[...].astype(F32)
    )
    root = bits[0:1]
    leaf = 2.0 * root + jnp.where(root > 0.5, bits[2:3], bits[1:2])
    w = w_ref[...]
    t = t_ref[...]
    y = y_ref[...]
    carried = jnp.concatenate(
        [w, w * t * t, w * t * y, leaf, jnp.zeros((4, rows), F32)], 0
    )
    node = node_ref[...]
    slot_hot = (iota((2 * cap, rows), 0) == code_ref[...].astype(jnp.int32)).astype(F32).astype(BF)
    pair = jnp.broadcast_to(node // 2, (8, rows))
    spread = jnp.concatenate(
        [jnp.where(pair == p, carried, 0.0) for p in range(nodes // 2)], 0
    ).astype(BF)
    moved = lax.dot_general(spread, slot_hot, NT, preferred_element_type=F32).astype(BF)
    for p in range(nodes // 2):
        piece = moved[p * 8 : (p + 1) * 8]
        part_ref[2 * p] = piece[:, :cap]
        part_ref[2 * p + 1] = piece[:, cap:]
    copy = pltpu.make_async_copy(part_ref, out_ref.at[:, pl.ds(out_ref.shape[1] - 8, 8), :], sem)
    copy.start()
    copy.wait()


HI = 4
LO = BINS // HI


def hist_kernel(
    got_ref, node_ref, child_ref, leaf_ref, hi_ref, lo_ref, w_ref, half0_ref, half1_ref
):
    halves = (half0_ref, half1_ref)
    sources, depth, cap = got_ref.shape
    feats = depth - 8
    cols = leaf_ref.shape[0] // feats
    slots = sources * cap
    for s in range(sources):
        at = slice(s * cap, (s + 1) * cap)
        x = got_ref[s, :feats, :].astype(F32)
        hi = jnp.floor(x * (1.0 / LO))
        hi_ref[:, at] = hi
        lo_ref[:, at] = x - hi * LO
        tail = got_ref[s, feats:, :].astype(F32)
        position = jnp.broadcast_to(tail[3:4], (3, cap))
        columns = jnp.concatenate(
            [jnp.where(position == float(q), tail[:3], 0.0) for q in range(cols // 3)], 0
        )
        w_ref[:, at] = jnp.concatenate([columns] * HI, 0).astype(BF)
    hi_of = (iota((HI * cols, slots), 0) // cols).astype(F32).astype(BF)
    lo_of = iota((LO, slots), 0).astype(F32).astype(BF)
    one = jnp.ones((), BF)
    zero = jnp.zeros((), BF)

    def step(f, carry):
        hi = jnp.broadcast_to(hi_ref[pl.ds(f, 1), :], (HI * cols, slots)).astype(BF)
        lo = jnp.broadcast_to(lo_ref[pl.ds(f, 1), :], (LO, slots)).astype(BF)
        a = jnp.where(hi == hi_of, w_ref[...], zero)
        b = jnp.where(lo == lo_of, one, zero)
        res = lax.dot_general(a, b, NT, preferred_element_type=F32)
        for half in range(2):
            parts = [res[h * cols : (h + 1) * cols] for h in (2 * half, 2 * half + 1)]
            halves[half][pl.ds(f, cols, stride=feats), :] = jnp.concatenate(parts, 1)
        return carry

    lax.fori_loop(0, feats, step, 0)
    size = 3 * feats
    leaf_ref[:, : BINS // 2] = half0_ref[...]
    leaf_ref[:, BINS // 2 :] = half1_ref[...]
    for c in range(cols // 6):
        child_ref[c * size : (c + 1) * size, :] = (
            leaf_ref[2 * c * size : (2 * c + 1) * size, :]
            + leaf_ref[(2 * c + 1) * size : (2 * c + 2) * size, :]
        )
    node_ref[...] = child_ref[:size, :] + child_ref[size:, :]


def vmem(n):
    return [pl.BlockSpec(memory_space=pltpu.VMEM)] * n


def on_device(
    binned,
    node_index,
    treatment,
    outcome,
    unit_weight,
    root_feature,
    root_cutoff,
    child_feature,
    child_cutoff,
):
    rows, feats = binned.shape
    nodes = root_feature.shape[0]
    owners = lax.axis_size("rows")
    feat_devices = lax.axis_size("feat")
    cap = 2 * rows // nodes
    depth = feats + 8
    params = pltpu.CompilerParams(vmem_limit_bytes=48 << 20)
    bins = binned.T
    node = node_index.T
    where = lax.axis_index("feat").astype(jnp.int32)[None]
    own = pl.pallas_call(
        split_kernel,
        out_shape=jax.ShapeDtypeStruct((8, rows), BF),
        in_specs=[pl.BlockSpec(memory_space=pltpu.SMEM)] + vmem(6),
        out_specs=vmem(1)[0],
        compiler_params=params,
        name="split",
    )(where, bins, node, root_feature[None], root_cutoff[None], child_feature[None], child_cutoff[None])
    others = [
        lax.ppermute(own, "feat", [(i, (i + k) % feat_devices) for i in range(feat_devices)])
        for k in range(1, feat_devices)
    ]
    buf, code = pl.pallas_call(
        place_kernel,
        out_shape=[
            jax.ShapeDtypeStruct((nodes, depth, cap), BF),
            jax.ShapeDtypeStruct((1, rows), F32),
        ],
        in_specs=vmem(2),
        out_specs=vmem(2),
        scratch_shapes=[pltpu.VMEM((nodes // 2 * feats, rows), BF)],
        compiler_params=params,
        name="place",
    )(bins, node)
    buf = pl.pallas_call(
        value_kernel,
        out_shape=jax.ShapeDtypeStruct((nodes, depth, cap), BF),
        in_specs=vmem(9) + [pl.BlockSpec(memory_space=pl.ANY)],
        out_specs=pl.BlockSpec(memory_space=pl.ANY),
        scratch_shapes=[pltpu.VMEM((nodes, 8, cap), BF), pltpu.SemaphoreType.DMA],
        input_output_aliases={9: 0},
        compiler_params=params,
        name="value",
    )(own, *others, node, code, unit_weight[None], treatment[None], outcome[None], buf)
    got = lax.all_to_all(buf, "rows", 0, 0, tiled=True)
    shape = lambda n: jax.ShapeDtypeStruct((n * 3 * feats, BINS), F32)
    node_moments, child_moments, leaf_moments = pl.pallas_call(
        hist_kernel,
        out_shape=[shape(1), shape(2), shape(4)],
        in_specs=vmem(1),
        out_specs=vmem(3),
        scratch_shapes=[
            pltpu.VMEM((feats, owners * cap), F32),
            pltpu.VMEM((feats, owners * cap), F32),
            pltpu.VMEM((HI * 12, owners * cap), BF),
            pltpu.VMEM((12 * feats, BINS // 2), F32),
            pltpu.VMEM((12 * feats, BINS // 2), F32),
        ],
        compiler_params=params,
        name="hist",
    )(got)
    return (
        node_moments.reshape(1, 3, feats, BINS),
        child_moments.reshape(2, 3, feats, BINS),
        leaf_moments.reshape(4, 3, feats, BINS),
    )


def solution(mesh):
    in_specs = (
        P("rows", "feat"),
        P("rows", None),
        P("rows"),
        P("rows"),
        P("rows"),
        P(),
        P(),
        P(),
        P(),
    )
    out_specs = (
        P("rows", None, "feat", None),
        P("rows", None, "feat", None),
        P("rows", None, "feat", None),
    )
    return jax.shard_map(
        on_device, mesh=mesh, in_specs=in_specs, out_specs=out_specs, check_vma=False
    )
```

time: 442 us -> 58.7 us (0.13)
  other arithmetic: 221 us -> 0 us
  matrix products: 104 us -> 0 us
  local copies, waits for them, and re-layouts: 52.5 us -> 1.74 us
  Pallas kernels: 0 us -> 27.3 us
  starting transfers between devices: 19.8 us -> 4.67 us
  between operations: 14.4 us -> 0.72 us
  waiting for transfers between devices: 11.5 us -> 1.94 us
  blocking collectives: 14.4 us -> 22.1 us
    gather x13 -> x0, other arithmetic: 200 us -> none  [the longest x2 40.3 us: on_device(): child_cutoff[first_child + 1]]
    dot_general x32 -> x0, matrix products: 104 us -> none  [one_block(): jnp.einsum('sc,fsb->cfb', weighted, table, preferred_element_type=jnp.flo...]
    pallas_call x0 -> x4, Pallas kernels: none -> 27.3 us  [the longest x1 24.7 us: on_device(): pl.pallas_call(hist_kernel, out_shape=[shape(1), shape(2), shape(4)], in_...]
    all_to_all x0 -> x1, blocking collectives: none -> 22.1 us  [on_device(): got = lax.all_to_all(buf, 'rows', 0, 0, tiled=True)]
    all_to_all x2 -> x0, starting transfers between devices: 19.7 us -> none  [the longest x1 12.3 us: on_device(): lax.all_to_all(moment_buffer, 'rows', split_axis=1, concat_axis=1, tiled=...]
    psum x1 -> x0, blocking collectives: 14.4 us -> none  [on_device(): lax.psum(picked.astype(jnp.float32), 'feat').astype(jnp.int32)]
    scatter x2 -> x0, local copies, waits for them, and re-layouts: 12.1 us -> none  [the longest x1 6.07 us: on_device(): jnp.zeros((4, node_count * capacity), jnp.bfloat16).at[:, slot_index]]
    all_to_all x2 -> x0, waiting for transfers between devices: 11.5 us -> none  [the longest x1 11.5 us: on_device(): lax.all_to_all(feat_buffer, 'rows', split_axis=1, concat_axis=1, tiled=True)]
  transfers between devices with their start and end apart: 3 -> 3, of which waited for: 1 -> 2; matrix products, arithmetic and copies ran while one was open for 68% -> 0% of each run, Pallas kernels for 0% -> 3%
where the time goes in v1:
time: 58.7 us; the launch traced here: 58.5 us
  Pallas kernels  27.3 us (47%)
  blocking collectives  22.1 us (38%)
  starting transfers between devices  4.67 us (8%)
  waiting for transfers between devices  1.94 us (3%)
  local copies, waits for them, and re-layouts  1.74 us (3%)
  between operations  0.72 us (1%)
    pallas_call x1, Pallas kernels, on_device(): pl.pallas_call(hist_kernel, out_shape=[shape(1), shape(2), shape(4)], in_...  24.7 us
    all_to_all x1, blocking collectives, on_device(): got = lax.all_to_all(buf, 'rows', 0, 0, tiled=True)  22.1 us
    ppermute x3, starting transfers between devices, on_device(): lax.ppermute(own, 'feat', [(i, (i + k) % feat_devices) for i in range(fea...  4.67 us
    ppermute x3, waiting for transfers between devices, on_device(): lax.ppermute(own, 'feat', [(i, (i + k) % feat_devices) for i in range(fea...  1.94 us
    unnamed x20, local copies, waits for them, and re-layouts  1.74 us
    pallas_call x1, Pallas kernels, on_device(): pl.pallas_call(place_kernel, out_shape=[jax.ShapeDtypeStruct((nodes, dept...  1.6 us
  transfers between devices with their start and end apart: 3, of which 2 were waited for; matrix products, arithmetic and copies ran while one was open for 0% of the time, Pallas kernels for 3%

profile of v1, /device:TPU:1, one launch (start us, length us, event | category | flops | bytes accessed | tf_op | source)
XLA Modules:
  0.0 58.5 jit_solution(12037970177777456918)
XLA Ops:
  0.6 0.0 copy-start.2
  0.6 0.0 copy-start.9
  0.7 0.0 copy-start.6
  0.7 0.0 copy-start.7
  0.7 0.0 copy-start.8
  0.7 0.6 %copy-done.2 = s32[2048,1]{0,1:T(1,128)S(1)} copy-done((s32[2048,1]{0,1:T(1,128)S(1)}, s32[2048,1]{0,1:T(1,128)}, u32[]{:S(2)}) %copy-start.2) | copy-done | bytes 8216
  1.3 0.0 copy-done.9
  1.3 0.0 copy-done.6
  1.3 0.0 copy-done.7
  1.3 0.0 copy-done.8
  1.4 0.0 copy-start
  1.4 1.0 %copy-done = s32[2048,64]{0,1:T(8,128)S(1)} copy-done((s32[2048,64]{0,1:T(8,128)S(1)}, s32[2048,64]{0,1:T(8,128)}, u32[]{:S(2)}) %copy-start) | copy-done | bytes 524312
  2.4 0.0 copy-start.1
  2.4 0.5 split.1.b0_ref
  2.9 3.6 %collective-permute-start.2 = (bf16[8,2048]{1,0:T(8,128)(2,1)S(1)}, bf16[8,2048]{1,0:T(8,128)(2,1)S(1)}, u32[]{:S(2)}, u32[]{:S(2)}) collective-permute-start(bf16[8,2048]{1,0:T(8,128)(2,1)S(1)} %split.1.b0_ref), channel_id=1, source_target_pairs={{0,3},{1,0},{2,1},{3,2},{4,7},{5,4},{6,5},{7,6},{8,11},{9,8},{10,9... | collective-permute-start | bytes 98312 | tf_op jit(solution)/shard_map/ppermute | solution.py:191
  6.5 0.4 collective-permute-start.1
  6.9 0.7 %collective-permute-start = (bf16[8,2048]{1,0:T(8,128)(2,1)S(1)}, bf16[8,2048]{1,0:T(8,128)(2,1)S(1)}, u32[]{:S(2)}, u32[]{:S(2)}) collective-permute-start(bf16[8,2048]{1,0:T(8,128)(2,1)S(1)} %split.1.b0_ref), channel_id=1, source_target_pairs={{0,1},{1,2},{2,3},{3,0},{4,5},{5,6},{6,7},{7,4},{8,9},{9,10},{10,1... | collective-permute-start | bytes 98312 | tf_op jit(solution)/shard_map/ppermute | solution.py:191
  7.6 0.0 copy-done.1
  7.6 0.0 copy-start.4
  7.6 0.0 copy-start.5
  7.6 1.6 %place.1 = (bf16[32,72,128]{2,1,0:T(8,128)(2,1)S(1)}, f32[1,2048]{1,0:T(1,128)S(1)}) custom-call(s32[64,2048]{1,0:T(8,128)S(1)} %bitcast.14, s32[1,2048]{1,0:T(1,128)S(1)} %bitcast.16), custom_call_target="tpu_custom_call" | custom-call | tf_op jit(solution)/shard_map/place/pallas_call | solution.py:194
  9.2 0.0 copy-start.3
  9.2 0.0 collective-permute-done.2.b3_ref
  9.2 1.6 %collective-permute-done.1.b2_ref = bf16[8,2048]{1,0:T(8,128)(2,1)S(1)} collective-permute-done((bf16[8,2048]{1,0:T(8,128)(2,1)S(1)}, bf16[8,2048]{1,0:T(8,128)(2,1)S(1)}, u32[]{:S(2)}, u32[]{:S(2)}) %collective-permute-start.1) | collective-permute-done | bytes 32800 | tf_op jit(solution)/shard_map/ppermute | solution.py:191
  10.8 0.3 collective-permute-done.b1_ref
  11.1 0.0 copy-done.4
  11.1 0.0 copy-done.5
  11.1 0.0 copy-done.3
  11.1 0.5 value.1
  11.7 22.1 %all_to_all.5.got_ref = bf16[32,72,128]{2,1,0:T(8,128)(2,1)S(1)} all-to-all(bf16[32,72,128]{2,1,0:T(8,128)(2,1)S(1)} %value.1), channel_id=1, replica_groups=mesh['rows'=32,'feat'=4] {'rows'}, dimensions={0} | all-to-all | bytes 1179648 | tf_op jit(solution)/shard_map/all_to_all | solution.py:216
  33.8 24.7 %hist.1 = (f32[192,256]{1,0:T(8,128)}, f32[384,256]{1,0:T(8,128)}, f32[768,256]{1,0:T(8,128)}) custom-call(bf16[32,72,128]{2,1,0:T(8,128)(2,1)S(1)} %all_to_all.5.got_ref), custom_call_target="tpu_custom_call" | custom-call | tf_op jit(solution)/shard_map/hist/pallas_call | solution.py:218
Async XLA Ops:
  0.6 0.7 %copy-start.2 = (s32[2048,1]{0,1:T(1,128)S(1)}, s32[2048,1]{0,1:T(1,128)}, u32[]{:S(2)}) copy-start(s32[2048,1]{0,1:T(1,128)} %param.10) | copy-start | bytes 24580
  0.6 0.7 %copy-start.9 = (s32[64]{0:T(128)S(1)}, s32[64]{0:T(128)}, u32[]{:S(2)}) copy-start(s32[64]{0:T(128)} %param.17) | copy-start | bytes 772
  0.7 0.7 %copy-start.6 = (s32[32]{0:T(128)S(1)}, s32[32]{0:T(128)}, u32[]{:S(2)}) copy-start(s32[32]{0:T(128)} %param.14) | copy-start | bytes 388
  0.7 0.7 %copy-start.7 = (s32[32]{0:T(128)S(1)}, s32[32]{0:T(128)}, u32[]{:S(2)}) copy-start(s32[32]{0:T(128)} %param.15) | copy-start | bytes 388
  0.7 0.7 %copy-start.8 = (s32[64]{0:T(128)S(1)}, s32[64]{0:T(128)}, u32[]{:S(2)}) copy-start(s32[64]{0:T(128)} %param.16) | copy-start | bytes 772
  1.4 1.0 %copy-start = (s32[2048,64]{0,1:T(8,128)S(1)}, s32[2048,64]{0,1:T(8,128)}, u32[]{:S(2)}) copy-start(s32[2048,64]{0,1:T(8,128)} %param.9) | copy-start | bytes 1572868
  2.4 5.2 %copy-start.1 = (s32[2048,64]{0,1:T(8,128)S(1)}, s32[2048,64]{0,1:T(8,128)}, u32[]{:S(2)}) copy-start(s32[2048,64]{0,1:T(8,128)} %param.9) | copy-start | bytes 1572868
  2.9 6.3 %collective-permute-start.2 = (bf16[8,2048]{1,0:T(8,128)(2,1)S(1)}, bf16[8,2048]{1,0:T(8,128)(2,1)S(1)}, u32[]{:S(2)}, u32[]{:S(2)}) collective-permute-start(bf16[8,2048]{1,0:T(8,128)(2,1)S(1)} %split.1.b0_ref), channel_id=1, source_target_pairs={{0,3},{1,0},{2,1},{3,2},{4,7},{5,4},{6,5},{7,6},{8,11},{9,8},{10,9... | collective-permute-start | bytes 98312 | tf_op jit(solution)/shard_map/ppermute | solution.py:191
  6.5 4.3 %collective-permute-start.1 = (bf16[8,2048]{1,0:T(8,128)(2,1)S(1)}, bf16[8,2048]{1,0:T(8,128)(2,1)S(1)}, u32[]{:S(2)}, u32[]{:S(2)}) collective-permute-start(bf16[8,2048]{1,0:T(8,128)(2,1)S(1)} %split.1.b0_ref), channel_id=1, source_target_pairs={{0,2},{1,3},{2,0},{3,1},{4,6},{5,7},{6,4},{7,5},{8,10},{9,11},{10,... | collective-permute-start | bytes 98312 | tf_op jit(solution)/shard_map/ppermute | solution.py:191
  6.9 4.3 %collective-permute-start = (bf16[8,2048]{1,0:T(8,128)(2,1)S(1)}, bf16[8,2048]{1,0:T(8,128)(2,1)S(1)}, u32[]{:S(2)}, u32[]{:S(2)}) collective-permute-start(bf16[8,2048]{1,0:T(8,128)(2,1)S(1)} %split.1.b0_ref), channel_id=1, source_target_pairs={{0,1},{1,2},{2,3},{3,0},{4,5},{5,6},{6,7},{7,4},{8,9},{9,10},{10,1... | collective-permute-start | bytes 98312 | tf_op jit(solution)/shard_map/ppermute | solution.py:191
  7.6 3.6 %copy-start.4 = (f32[2048]{0:T(1024)S(1)}, f32[2048]{0:T(1024)}, u32[]{:S(2)}) copy-start(f32[2048]{0:T(1024)} %param.11) | copy-start | bytes 24580
  7.6 3.6 %copy-start.5 = (f32[2048]{0:T(1024)S(1)}, f32[2048]{0:T(1024)}, u32[]{:S(2)}) copy-start(f32[2048]{0:T(1024)} %param.12) | copy-start | bytes 24580
  9.2 2.0 %copy-start.3 = (f32[2048]{0:T(1024)S(1)}, f32[2048]{0:T(1024)}, u32[]{:S(2)}) copy-start(f32[2048]{0:T(1024)} %param.13) | copy-start | bytes 24580

commit v2 on v1

v2 whole, which is shorter than its diff:
```python
import jax
import jax.numpy as jnp
from jax import lax
from jax.experimental import pallas as pl
from jax.experimental.pallas import tpu as pltpu
from jax.sharding import PartitionSpec as P

BINS = 256
BF = jnp.bfloat16
F32 = jnp.float32
NT = (((1,), (1,)), ((), ()))
NN = (((1,), (0,)), ((), ()))
HI = 4
LO = BINS // HI


def iota(shape, axis):
    return lax.broadcasted_iota(jnp.int32, shape, axis)


def place_kernel(
    owner_ref, place_ref, rf_ref, rc_ref, cf_ref, cc_ref, bins_hbm, node_hbm, w_hbm, t_hbm, y_hbm,
    out_ref, split_ref, bins_ref, node_ref, w_ref, t_ref, y_ref, a_ref, sems,
):
    copies = [
        pltpu.make_async_copy(source, target, sems.at[i])
        for i, (source, target) in enumerate(
            zip((node_hbm, w_hbm, t_hbm, y_hbm, bins_hbm), (node_ref, w_ref, t_ref, y_ref, bins_ref))
        )
    ]
    for copy in copies:
        copy.start()
    feats, rows = bins_ref.shape
    nodes, depth, cap = out_ref.shape
    blocks = rows // 256
    own = owner_ref[0]
    first = place_ref[0] * feats
    table = [
        rf_ref[own] - first, cf_ref[2 * own] - first, cf_ref[2 * own + 1] - first,
        rc_ref[own], cc_ref[2 * own], cc_ref[2 * own + 1],
    ]
    for k, entry in enumerate(table):
        split_ref[k : k + 1, :] = jnp.full((1, cap), entry, jnp.int32)
    copies[0].wait()
    node = node_ref[...]
    hot = (iota((nodes, rows), 0) == node).astype(F32)
    stacked = jnp.concatenate([hot[:, b * 256 : (b + 1) * 256] for b in range(blocks)], 0)
    before = (iota((256, 256), 0) < iota((256, 256), 1)).astype(F32).astype(BF)
    ones = jnp.ones((256, 256), BF)
    inner = lax.dot_general(stacked.astype(BF), before, NN, preferred_element_type=F32)
    total = lax.dot_general(stacked.astype(BF), ones, NN, preferred_element_type=F32)
    carry = jnp.zeros((nodes, 256), F32)
    ranks = []
    for b in range(blocks):
        part = slice(b * nodes, (b + 1) * nodes)
        ranks.append(jnp.sum(stacked[part] * (inner[part] + carry), 0, keepdims=True))
        carry = carry + total[part]
    rank = jnp.concatenate(ranks, 1)
    code = rank.astype(jnp.int32) + node % 2 * cap
    slot_hot = (iota((2 * cap, rows), 0) == code).astype(F32).astype(BF)
    for copy in copies[1:4]:
        copy.wait()
    w = w_ref[...]
    t = t_ref[...]
    y = y_ref[...]
    carried = jnp.concatenate([w, w * t * t, w * t * y, jnp.zeros((depth - feats - 3, rows), F32)], 0)
    copies[4].wait()
    bins = jnp.concatenate([bins_ref[...].astype(F32), carried], 0).astype(BF)
    pair = jnp.broadcast_to(node // 2, (depth, rows))
    for p in range(nodes // 2):
        a_ref[p * depth : (p + 1) * depth, :] = jnp.where(pair == p, bins, jnp.zeros((), BF))
    moved = lax.dot_general(a_ref[...], slot_hot, NT, preferred_element_type=F32).astype(BF)
    for p in range(nodes // 2):
        piece = moved[p * depth : (p + 1) * depth]
        out_ref[2 * p] = piece[:, :cap]
        out_ref[2 * p + 1] = piece[:, cap:]


def split_kernel(split_ref, got_ref, bits_ref):
    sources, depth, cap = got_ref.shape
    feats = depth - 8
    feature = iota((feats, cap), 0)
    masks = [feature == split_ref[k : k + 1, :] for k in range(3)]
    cutoffs = [split_ref[k : k + 1, :].astype(F32) for k in range(3, 6)]
    rows = [[], [], []]
    for s in range(sources):
        x = got_ref[s, :feats, :].astype(F32)
        for k in range(3):
            right = jnp.where(jnp.logical_and(masks[k], x > cutoffs[k]), 1.0, 0.0)
            rows[k].append(jnp.sum(right, 0, keepdims=True))
    for k in range(3):
        bits_ref[k] = jnp.concatenate(rows[k], 0).astype(BF)


def hist_kernel(
    got_ref, b0_ref, b1_ref, b2_ref, b3_ref, node_ref, child_ref, leaf_ref, hi_ref, lo_ref, w_ref,
    half0_ref, half1_ref,
):
    sources, depth, cap = got_ref.shape
    feats = depth - 8
    cols = leaf_ref.shape[0] // feats
    halves = (half0_ref, half1_ref)
    bits = (b0_ref[...].astype(F32) + b1_ref[...].astype(F32)) + (
        b2_ref[...].astype(F32) + b3_ref[...].astype(F32)
    )
    leaf = 2.0 * bits[0] + jnp.where(bits[0] > 0.5, bits[2], bits[1])
    for s in range(sources):
        x = got_ref[s, :feats, :].astype(F32)
        hi = jnp.floor(x * (1.0 / LO))
        hi_ref[s * feats : (s + 1) * feats, :] = hi
        lo_ref[s * feats : (s + 1) * feats, :] = x - hi * LO
        tail = got_ref[s, feats:, :].astype(F32)
        position = jnp.broadcast_to(leaf[s : s + 1], (3, cap))
        columns = jnp.concatenate(
            [jnp.where(position == float(q), tail[:3], 0.0) for q in range(cols // 3)], 0
        )
        w_ref[:, s * cap : (s + 1) * cap] = jnp.concatenate([columns] * HI, 0).astype(BF)
    hi_of = [((iota((16, cap), 0) + 16 * i) // cols).astype(F32).astype(BF) for i in range(HI * cols // 16)]
    lo_of = [(iota((16, cap), 0) + 16 * i).astype(F32).astype(BF) for i in range(LO // 16)]
    one = jnp.ones((), BF)
    zero = jnp.zeros((), BF)

    def step(f, carry):
        res = None
        for k in range(sources // 2):
            a = []
            b = []
            for s in (2 * k, 2 * k + 1):
                hi = hi_ref[pl.ds(s * feats + f, 16, stride=0), :].astype(BF)
                lo = lo_ref[pl.ds(s * feats + f, 16, stride=0), :].astype(BF)
                w = w_ref[:, s * cap : (s + 1) * cap]
                a.append(
                    jnp.concatenate(
                        [jnp.where(hi == of, w[i * 16 : (i + 1) * 16], zero) for i, of in enumerate(hi_of)], 0
                    )
                )
                b.append(jnp.concatenate([jnp.where(lo == of, one, zero) for of in lo_of], 0))
            part = lax.dot_general(
                jnp.concatenate(a, 1), jnp.concatenate(b, 1), NT, preferred_element_type=F32
            )
            res = part if res is None else res + part
        for half in range(2):
            parts = [res[h * cols : (h + 1) * cols] for h in (2 * half, 2 * half + 1)]
            halves[half][pl.ds(f, cols, stride=feats), :] = jnp.concatenate(parts, 1)
        return carry

    lax.fori_loop(0, feats, step, 0, unroll=4)
    size = 3 * feats
    leaf_ref[:, : BINS // 2] = half0_ref[...]
    leaf_ref[:, BINS // 2 :] = half1_ref[...]
    for c in range(cols // 6):
        child_ref[c * size : (c + 1) * size, :] = (
            leaf_ref[2 * c * size : (2 * c + 1) * size, :]
            + leaf_ref[(2 * c + 1) * size : (2 * c + 2) * size, :]
        )
    node_ref[...] = child_ref[:size, :] + child_ref[size:, :]


def specs(space, n):
    return [pl.BlockSpec(memory_space=space)] * n


def on_device(
    binned,
    node_index,
    treatment,
    outcome,
    unit_weight,
    root_feature,
    root_cutoff,
    child_feature,
    child_cutoff,
):
    rows, feats = binned.shape
    nodes = root_feature.shape[0]
    owners = lax.axis_size("rows")
    feat_devices = lax.axis_size("feat")
    cap = 2 * rows // nodes
    depth = feats + 8
    params = pltpu.CompilerParams(vmem_limit_bytes=48 << 20)
    here = lambda name: lax.axis_index(name).astype(jnp.int32)[None]
    rowwise = [binned.T, node_index.T, unit_weight[None], treatment[None], outcome[None]]
    buf, splits = pl.pallas_call(
        place_kernel,
        out_shape=[
            jax.ShapeDtypeStruct((nodes, depth, cap), BF),
            jax.ShapeDtypeStruct((8, cap), jnp.int32),
        ],
        in_specs=specs(pltpu.SMEM, 6) + specs(pltpu.HBM, 5),
        out_specs=specs(pltpu.VMEM, 2),
        scratch_shapes=[
            pltpu.VMEM((feats, rows), jnp.int32),
            pltpu.VMEM((1, rows), jnp.int32),
            pltpu.VMEM((1, rows), F32),
            pltpu.VMEM((1, rows), F32),
            pltpu.VMEM((1, rows), F32),
            pltpu.VMEM((nodes // 2 * depth, rows), BF),
            pltpu.SemaphoreType.DMA((5,)),
        ],
        compiler_params=params,
        name="place",
    )(
        here("rows"), here("feat"), root_feature, root_cutoff, child_feature, child_cutoff,
        *[pltpu.with_memory_space_constraint(x, pltpu.HBM) for x in rowwise],
    )
    got = lax.all_to_all(buf, "rows", 0, 0, tiled=True)
    own = pl.pallas_call(
        split_kernel,
        out_shape=jax.ShapeDtypeStruct((3, owners, cap), BF),
        in_specs=specs(pltpu.VMEM, 2),
        out_specs=specs(pltpu.VMEM, 1)[0],
        compiler_params=params,
        name="split",
    )(splits, got)
    others = [
        lax.ppermute(own, "feat", [(i, (i + k) % feat_devices) for i in range(feat_devices)])
        for k in range(1, feat_devices)
    ]
    shape = lambda n: jax.ShapeDtypeStruct((n * 3 * feats, BINS), F32)
    node_moments, child_moments, leaf_moments = pl.pallas_call(
        hist_kernel,
        out_shape=[shape(1), shape(2), shape(4)],
        in_specs=specs(pltpu.VMEM, 5),
        out_specs=specs(pltpu.VMEM, 3),
        scratch_shapes=[
            pltpu.VMEM((owners * feats, cap), F32),
            pltpu.VMEM((owners * feats, cap), F32),
            pltpu.VMEM((HI * 12, owners * cap), BF),
            pltpu.VMEM((12 * feats, BINS // 2), F32),
            pltpu.VMEM((12 * feats, BINS // 2), F32),
        ],
        compiler_params=params,
        name="hist",
    )(got, own, *others)
    return (
        node_moments.reshape(1, 3, feats, BINS),
        child_moments.reshape(2, 3, feats, BINS),
        leaf_moments.reshape(4, 3, feats, BINS),
    )


def solution(mesh):
    in_specs = (
        P("rows", "feat"),
        P("rows", None),
        P("rows"),
        P("rows"),
        P("rows"),
        P(),
        P(),
        P(),
        P(),
    )
    out_specs = (
        P("rows", None, "feat", None),
        P("rows", None, "feat", None),
        P("rows", None, "feat", None),
    )
    return jax.shard_map(
        on_device, mesh=mesh, in_specs=in_specs, out_specs=out_specs, check_vma=False
    )
```

time: 58.7 us -> 48.4 us (0.82)
  Pallas kernels: 27.3 us -> 17.7 us
  waiting for transfers between devices: 1.94 us -> 3.78 us
  local copies, waits for them, and re-layouts: 1.74 us -> 0.67 us
  starting transfers between devices: 4.67 us -> 3.84 us
  blocking collectives: 22.1 us -> 21.5 us
    pallas_call x1, Pallas kernels: 24.7 us -> 13.9 us  [on_device(): pl.pallas_call(hist_kernel, out_shape=[shape(1), shape(2), shape(4)], in_...]
    ppermute x3, waiting for transfers between devices: 1.94 us -> 3.78 us  [on_device(): lax.ppermute(own, 'feat', [(i, (i + k) % feat_devices) for i in range(fea...]
    pallas_call x1, Pallas kernels: 1.6 us -> 3.32 us  [on_device(): pl.pallas_call(place_kernel, out_shape=[jax.ShapeDtypeStruct((nodes, dept...]
    unnamed x20 -> x8, local copies, waits for them, and re-layouts: 1.74 us -> 0.67 us
    ppermute x3, starting transfers between devices: 4.67 us -> 3.84 us  [on_device(): lax.ppermute(own, 'feat', [(i, (i + k) % feat_devices) for i in range(fea...]
    all_to_all x1, blocking collectives: 22.1 us -> 21.5 us  [on_device(): got = lax.all_to_all(buf, 'rows', 0, 0, tiled=True)]
  transfers between devices with their start and end apart: 3 -> 3, of which waited for: 2 -> 2; matrix products, arithmetic and copies ran while one was open for 0% -> 0% of each run, Pallas kernels for 3% -> 0%
where the time goes in v2:
time: 48.4 us; the launch traced here: 48.2 us
  blocking collectives  21.5 us (44%)
  Pallas kernels  17.7 us (37%)
  starting transfers between devices  3.84 us (8%)
  waiting for transfers between devices  3.78 us (8%)
  between operations  0.69 us (1%)
  local copies, waits for them, and re-layouts  0.67 us (1%)
    all_to_all x1, blocking collectives, on_device(): got = lax.all_to_all(buf, 'rows', 0, 0, tiled=True)  21.5 us
    pallas_call x1, Pallas kernels, on_device(): pl.pallas_call(hist_kernel, out_shape=[shape(1), shape(2), shape(4)], in_...  13.9 us
    ppermute x3, starting transfers between devices, on_device(): lax.ppermute(own, 'feat', [(i, (i + k) % feat_devices) for i in range(fea...  3.84 us
    ppermute x3, waiting for transfers between devices, on_device(): lax.ppermute(own, 'feat', [(i, (i + k) % feat_devices) for i in range(fea...  3.78 us
    pallas_call x1, Pallas kernels, on_device(): pl.pallas_call(place_kernel, out_shape=[jax.ShapeDtypeStruct((nodes, dept...  3.32 us
  transfers between devices with their start and end apart: 3, of which 2 were waited for; matrix products, arithmetic and copies ran while one was open for 0% of the time, Pallas kernels for 0%

profile of v2, /device:TPU:1, one launch (start us, length us, event | category | flops | bytes accessed | tf_op | source)
XLA Modules:
  0.0 48.2 jit_solution(8787092988711440883)
XLA Ops:
  0.6 0.0 copy-start.3
  0.6 0.0 copy-start
  0.7 0.0 copy-start.1
  0.7 0.0 copy-start.2
  0.7 0.6 %copy-done.3 = s32[64]{0:T(128)S(1)} copy-done((s32[64]{0:T(128)S(1)}, s32[64]{0:T(128)}, u32[]{:S(2)}) %copy-start.3) | copy-done | bytes 280
  1.3 0.0 copy-done
  1.3 0.0 copy-done.1
  1.3 0.0 copy-done.2
  1.3 3.3 %place.1 = (bf16[32,72,128]{2,1,0:T(8,128)(2,1)S(1)}, s32[8,128]{1,0:T(8,128)S(1)}) custom-call(s32[1]{0:T(128)} %bitcast.owner_ref, s32[1]{0:T(128)} %bitcast.1.place_ref, s32[32]{0:T(128)S(1)} %copy-done, s32[32]{0:T(128)S(1)} %copy-done.1, s32[64]{0:T(128)S(1)} %copy-done.2, s32[64]{0:T(128)S(1)} %copy-done.3, s32[64,2048]{1,0:T(8,128)} %bitcast.10, ...), custom_call_target="tpu_custom_call" | custom-call | tf_op jit(solution)/shard_map/place/pallas_call | solution.py:183
  4.7 21.5 %all_to_all.5.got_ref = bf16[32,72,128]{2,1,0:T(8,128)(2,1)S(1)} all-to-all(bf16[32,72,128]{2,1,0:T(8,128)(2,1)S(1)} %get-tuple-element.8), channel_id=1, replica_groups=mesh['rows'=32,'feat'=4] {'rows'}, dimensions={0} | all-to-all | bytes 1179648 | tf_op jit(solution)/shard_map/all_to_all | solution.py:206
  26.2 0.5 %split.1.b0_ref = bf16[3,32,128]{2,1,0:T(8,128)(2,1)S(1)} custom-call(s32[8,128]{1,0:T(8,128)S(1)} %get-tuple-element.9.split_ref, bf16[32,72,128]{2,1,0:T(8,128)(2,1)S(1)} %all_to_all.5.got_ref), custom_call_target="tpu_custom_call" | custom-call | tf_op jit(solution)/shard_map/split/pallas_call | solution.py:207
  26.7 2.8 %collective-permute-start.2 = (bf16[3,32,128]{2,1,0:T(8,128)(2,1)S(1)}, bf16[3,32,128]{2,1,0:T(8,128)(2,1)S(1)}, u32[]{:S(2)}, u32[]{:S(2)}) collective-permute-start(bf16[3,32,128]{2,1,0:T(8,128)(2,1)S(1)} %split.1.b0_ref), channel_id=1, source_target_pairs={{0,3},{1,0},{2,1},{3,2},{4,7},{5,4},{6,5},{7,6},{8,11},{9,8},{10,9... | collective-permute-start | bytes 73736 | tf_op jit(solution)/shard_map/ppermute | solution.py:216
  29.5 0.3 collective-permute-start.1
  29.9 0.7 %collective-permute-start = (bf16[3,32,128]{2,1,0:T(8,128)(2,1)S(1)}, bf16[3,32,128]{2,1,0:T(8,128)(2,1)S(1)}, u32[]{:S(2)}, u32[]{:S(2)}) collective-permute-start(bf16[3,32,128]{2,1,0:T(8,128)(2,1)S(1)} %split.1.b0_ref), channel_id=1, source_target_pairs={{0,1},{1,2},{2,3},{3,0},{4,5},{5,6},{6,7},{7,4},{8,9},{9,10},{10,1... | collective-permute-start | bytes 73736 | tf_op jit(solution)/shard_map/ppermute | solution.py:216
  30.6 0.0 collective-permute-done.2.b3_ref
  30.6 3.2 %collective-permute-done.1.b2_ref = bf16[3,32,128]{2,1,0:T(8,128)(2,1)S(1)} collective-permute-done((bf16[3,32,128]{2,1,0:T(8,128)(2,1)S(1)}, bf16[3,32,128]{2,1,0:T(8,128)(2,1)S(1)}, u32[]{:S(2)}, u32[]{:S(2)}) %collective-permute-start.1) | collective-permute-done | bytes 24608 | tf_op jit(solution)/shard_map/ppermute | solution.py:216
  33.7 0.6 %collective-permute-done.b1_ref = bf16[3,32,128]{2,1,0:T(8,128)(2,1)S(1)} collective-permute-done((bf16[3,32,128]{2,1,0:T(8,128)(2,1)S(1)}, bf16[3,32,128]{2,1,0:T(8,128)(2,1)S(1)}, u32[]{:S(2)}, u32[]{:S(2)}) %collective-permute-start) | collective-permute-done | bytes 24608 | tf_op jit(solution)/shard_map/ppermute | solution.py:216
  34.3 13.9 %hist.1 = (f32[192,256]{1,0:T(8,128)}, f32[384,256]{1,0:T(8,128)}, f32[768,256]{1,0:T(8,128)}) custom-call(bf16[32,72,128]{2,1,0:T(8,128)(2,1)S(1)} %all_to_all.5.got_ref, bf16[3,32,128]{2,1,0:T(8,128)(2,1)S(1)} %split.1.b0_ref, bf16[3,32,128]{2,1,0:T(8,128)(2,1)S(1)} %collective-permute-done.b1_ref, bf16[3,32,128]{2,1,0:T(8,128)(2,1)S(1)} %collective-permute-done.1.b2_ref, ...), custom_call_target="tpu_custom_call" | custom-call | tf_op jit(solution)/shard_map/hist/pallas_call | solution.py:220
Async XLA Ops:
  0.6 0.7 %copy-start.3 = (s32[64]{0:T(128)S(1)}, s32[64]{0:T(128)}, u32[]{:S(2)}) copy-start(s32[64]{0:T(128)} %cc_ref.1) | copy-start | bytes 772
  0.6 0.7 %copy-start = (s32[32]{0:T(128)S(1)}, s32[32]{0:T(128)}, u32[]{:S(2)}) copy-start(s32[32]{0:T(128)} %rf_ref.1) | copy-start | bytes 388
  0.7 0.7 %copy-start.1 = (s32[32]{0:T(128)S(1)}, s32[32]{0:T(128)}, u32[]{:S(2)}) copy-start(s32[32]{0:T(128)} %rc_ref.1) | copy-start | bytes 388
  0.7 0.7 %copy-start.2 = (s32[64]{0:T(128)S(1)}, s32[64]{0:T(128)}, u32[]{:S(2)}) copy-start(s32[64]{0:T(128)} %cf_ref.1) | copy-start | bytes 772
  26.7 3.8 %collective-permute-start.2 = (bf16[3,32,128]{2,1,0:T(8,128)(2,1)S(1)}, bf16[3,32,128]{2,1,0:T(8,128)(2,1)S(1)}, u32[]{:S(2)}, u32[]{:S(2)}) collective-permute-start(bf16[3,32,128]{2,1,0:T(8,128)(2,1)S(1)} %split.1.b0_ref), channel_id=1, source_target_pairs={{0,3},{1,0},{2,1},{3,2},{4,7},{5,4},{6,5},{7,6},{8,11},{9,8},{10,9... | collective-permute-start | bytes 73736 | tf_op jit(solution)/shard_map/ppermute | solution.py:216
  29.5 4.2 %collective-permute-start.1 = (bf16[3,32,128]{2,1,0:T(8,128)(2,1)S(1)}, bf16[3,32,128]{2,1,0:T(8,128)(2,1)S(1)}, u32[]{:S(2)}, u32[]{:S(2)}) collective-permute-start(bf16[3,32,128]{2,1,0:T(8,128)(2,1)S(1)} %split.1.b0_ref), channel_id=1, source_target_pairs={{0,2},{1,3},{2,0},{3,1},{4,6},{5,7},{6,4},{7,5},{8,10},{9,11},{10,... | collective-permute-start | bytes 73736 | tf_op jit(solution)/shard_map/ppermute | solution.py:216
  29.9 4.5 %collective-permute-start = (bf16[3,32,128]{2,1,0:T(8,128)(2,1)S(1)}, bf16[3,32,128]{2,1,0:T(8,128)(2,1)S(1)}, u32[]{:S(2)}, u32[]{:S(2)}) collective-permute-start(bf16[3,32,128]{2,1,0:T(8,128)(2,1)S(1)} %split.1.b0_ref), channel_id=1, source_target_pairs={{0,1},{1,2},{2,3},{3,0},{4,5},{5,6},{6,7},{7,4},{8,9},{9,10},{10,1... | collective-permute-start | bytes 73736 | tf_op jit(solution)/shard_map/ppermute | solution.py:216

commit v3 on v2

--- a/solution.py
+++ b/solution.py
@@ -12,6 +12,8 @@
 NN = (((1,), (0,)), ((), ()))
 HI = 4
 LO = BINS // HI
+UNROLL = 16
+FINISH = 32
 
 
 def iota(shape, axis):
@@ -19,13 +21,18 @@
 
 
 def place_kernel(
-    owner_ref, place_ref, rf_ref, rc_ref, cf_ref, cc_ref, bins_hbm, node_hbm, w_hbm, t_hbm, y_hbm,
-    out_ref, split_ref, bins_ref, node_ref, w_ref, t_ref, y_ref, a_ref, sems,
+    owner_ref, place_ref, node_hbm, w_hbm, t_hbm, y_hbm, bins_hbm, rf_hbm, cf_hbm, rc_hbm, cc_hbm,
+    out_ref, split_ref, node_ref, w_ref, t_ref, y_ref, bins_ref, rf_ref, cf_ref, rc_ref, cc_ref,
+    a_ref, sems,
 ):
     copies = [
         pltpu.make_async_copy(source, target, sems.at[i])
         for i, (source, target) in enumerate(
-            zip((node_hbm, w_hbm, t_hbm, y_hbm, bins_hbm), (node_ref, w_ref, t_ref, y_ref, bins_ref))
+            (
+                (node_hbm, node_ref), (w_hbm, w_ref), (t_hbm, t_ref), (y_hbm, y_ref),
+                (bins_hbm, bins_ref), (rf_hbm, rf_ref), (cf_hbm, cf_ref), (rc_hbm, rc_ref),
+                (cc_hbm, cc_ref),
+            )
         )
     ]
     for copy in copies:
@@ -33,14 +40,6 @@
     feats, rows = bins_ref.shape
     nodes, depth, cap = out_ref.shape
     blocks = rows // 256
-    own = owner_ref[0]
-    first = place_ref[0] * feats
-    table = [
-        rf_ref[own] - first, cf_ref[2 * own] - first, cf_ref[2 * own + 1] - first,
-        rc_ref[own], cc_ref[2 * own], cc_ref[2 * own + 1],
-    ]
-    for k, entry in enumerate(table):
-        split_ref[k : k + 1, :] = jnp.full((1, cap), entry, jnp.int32)
     copies[0].wait()
     node = node_ref[...]
     hot = (iota((nodes, rows), 0) == node).astype(F32)
@@ -74,6 +73,16 @@
         piece = moved[p * depth : (p + 1) * depth]
         out_ref[2 * p] = piece[:, :cap]
         out_ref[2 * p + 1] = piece[:, cap:]
+    for copy in copies[5:]:
+        copy.wait()
+    own = owner_ref[0]
+    first = place_ref[0] * feats
+    table = [
+        rf_ref[own] - first, cf_ref[2 * own] - first, cf_ref[2 * own + 1] - first,
+        rc_ref[own], cc_ref[2 * own], cc_ref[2 * own + 1],
+    ]
+    for k, entry in enumerate(table):
+        split_ref[k : k + 1, :] = jnp.full((1, cap), entry, jnp.int32)
 
 
 def split_kernel(split_ref, got_ref, bits_ref):
@@ -92,23 +101,29 @@
         bits_ref[k] = jnp.concatenate(rows[k], 0).astype(BF)
 
 
-def hist_kernel(
-    got_ref, b0_ref, b1_ref, b2_ref, b3_ref, node_ref, child_ref, leaf_ref, hi_ref, lo_ref, w_ref,
-    half0_ref, half1_ref,
-):
-    sources, depth, cap = got_ref.shape
+def prepare_kernel(got_ref, hi_ref, lo_ref):
+    sources, depth, _ = got_ref.shape
     feats = depth - 8
-    cols = leaf_ref.shape[0] // feats
-    halves = (half0_ref, half1_ref)
-    bits = (b0_ref[...].astype(F32) + b1_ref[...].astype(F32)) + (
-        b2_ref[...].astype(F32) + b3_ref[...].astype(F32)
-    )
-    leaf = 2.0 * bits[0] + jnp.where(bits[0] > 0.5, bits[2], bits[1])
     for s in range(sources):
         x = got_ref[s, :feats, :].astype(F32)
         hi = jnp.floor(x * (1.0 / LO))
         hi_ref[s * feats : (s + 1) * feats, :] = hi
         lo_ref[s * feats : (s + 1) * feats, :] = x - hi * LO
+
+
+def hist_kernel(
+    got_ref, hi_ref, lo_ref, b0_ref, b1_ref, b2_ref, b3_ref, node_hbm, child_hbm, leaf_hbm, w_ref,
+    half0_ref, half1_ref, node_ref, child_ref, leaf_ref, sems,
+):
+    sources, depth, cap = got_ref.shape
+    feats = depth - 8
+    cols = leaf_ref.shape[0]
+    halves = (half0_ref, half1_ref)
+    bits = (b0_ref[...].astype(F32) + b1_ref[...].astype(F32)) + (
+        b2_ref[...].astype(F32) + b3_ref[...].astype(F32)
+    )
+    leaf = 2.0 * bits[0] + jnp.where(bits[0] > 0.5, bits[2], bits[1])
+    for s in range(sources):
         tail = got_ref[s, feats:, :].astype(F32)
         position = jnp.broadcast_to(leaf[s : s + 1], (3, cap))
         columns = jnp.concatenate(
@@ -144,16 +159,37 @@
             halves[half][pl.ds(f, cols, stride=feats), :] = jnp.concatenate(parts, 1)
         return carry
 
-    lax.fori_loop(0, feats, step, 0, unroll=4)
-    size = 3 * feats
-    leaf_ref[:, : BINS // 2] = half0_ref[...]
-    leaf_ref[:, BINS // 2 :] = half1_ref[...]
-    for c in range(cols // 6):
-        child_ref[c * size : (c + 1) * size, :] = (
-            leaf_ref[2 * c * size : (2 * c + 1) * size, :]
-            + leaf_ref[(2 * c + 1) * size : (2 * c + 2) * size, :]
-        )
-    node_ref[...] = child_ref[:size, :] + child_ref[size:, :]
+    def outputs(first):
+        at = pl.ds(first, FINISH)
+        return [
+            pltpu.make_async_copy(source.at[:, at, :], target.at[:, at, :], sems.at[first // FINISH, i])
+            for i, (source, target) in enumerate(
+                ((leaf_ref, leaf_hbm), (child_ref, child_hbm), (node_ref, node_hbm))
+            )
+        ]
+
+    def group(g, carry):
+        first = pl.multiple_of(g * FINISH, FINISH)
+        lax.fori_loop(0, FINISH, lambda i, c: step(first + i, c), 0, unroll=UNROLL)
+        at = pl.ds(first, FINISH)
+        for half in range(2):
+            lanes = slice(half * (BINS // 2), (half + 1) * (BINS // 2))
+            value = [halves[half][pl.ds(c * feats + first, FINISH), :] for c in range(cols)]
+            for c in range(cols):
+                leaf_ref[c, at, lanes] = value[c]
+            pairs = [value[c] + value[c + 3] for c in (0, 1, 2, 6, 7, 8)]
+            for c in range(6):
+                child_ref[c, at, lanes] = pairs[c]
+            for c in range(3):
+                node_ref[c, at, lanes] = pairs[c] + pairs[c + 3]
+        for copy in outputs(first):
+            copy.start()
+        return carry
+
+    lax.fori_loop(0, feats // FINISH, group, 0)
+    for g in range(feats // FINISH):
+        for copy in outputs(g * FINISH):
+            copy.wait()
 
 
 def specs(space, n):
@@ -177,31 +213,38 @@
     feat_devices = lax.axis_size("feat")
     cap = 2 * rows // nodes
     depth = feats + 8
-    params = pltpu.CompilerParams(vmem_limit_bytes=48 << 20)
+    params = pltpu.CompilerParams(vmem_limit_bytes=24 << 20)
     here = lambda name: lax.axis_index(name).astype(jnp.int32)[None]
-    rowwise = [binned.T, node_index.T, unit_weight[None], treatment[None], outcome[None]]
+    sources = [
+        node_index.T, unit_weight[None], treatment[None], outcome[None], binned.T,
+        root_feature, child_feature, root_cutoff, child_cutoff,
+    ]
     buf, splits = pl.pallas_call(
         place_kernel,
         out_shape=[
             jax.ShapeDtypeStruct((nodes, depth, cap), BF),
             jax.ShapeDtypeStruct((8, cap), jnp.int32),
         ],
-        in_specs=specs(pltpu.SMEM, 6) + specs(pltpu.HBM, 5),
+        in_specs=specs(pltpu.SMEM, 2) + specs(pltpu.HBM, 9),
         out_specs=specs(pltpu.VMEM, 2),
         scratch_shapes=[
-            pltpu.VMEM((feats, rows), jnp.int32),
             pltpu.VMEM((1, rows), jnp.int32),
             pltpu.VMEM((1, rows), F32),
             pltpu.VMEM((1, rows), F32),
             pltpu.VMEM((1, rows), F32),
+            pltpu.VMEM((feats, rows), jnp.int32),
+            pltpu.SMEM((nodes,), jnp.int32),
+            pltpu.SMEM((2 * nodes,), jnp.int32),
+            pltpu.SMEM((nodes,), jnp.int32),
+            pltpu.SMEM((2 * nodes,), jnp.int32),
             pltpu.VMEM((nodes // 2 * depth, rows), BF),
-            pltpu.SemaphoreType.DMA((5,)),
+            pltpu.SemaphoreType.DMA((9,)),
         ],
         compiler_params=params,
         name="place",
     )(
-        here("rows"), here("feat"), root_feature, root_cutoff, child_feature, child_cutoff,
-        *[pltpu.with_memory_space_constraint(x, pltpu.HBM) for x in rowwise],
+        here("rows"), here("feat"),
+        *[pltpu.with_memory_space_constraint(x, pltpu.HBM) for x in sources],
     )
     got = lax.all_to_all(buf, "rows", 0, 0, tiled=True)
     own = pl.pallas_call(
@@ -216,22 +259,32 @@
         lax.ppermute(own, "feat", [(i, (i + k) % feat_devices) for i in range(feat_devices)])
         for k in range(1, feat_devices)
     ]
-    shape = lambda n: jax.ShapeDtypeStruct((n * 3 * feats, BINS), F32)
+    digit = jax.ShapeDtypeStruct((owners * feats, cap), F32)
+    hi, lo = pl.pallas_call(
+        prepare_kernel,
+        out_shape=[digit, digit],
+        in_specs=specs(pltpu.VMEM, 1),
+        out_specs=specs(pltpu.VMEM, 2),
+        compiler_params=params,
+        name="prepare",
+    )(got)
     node_moments, child_moments, leaf_moments = pl.pallas_call(
         hist_kernel,
-        out_shape=[shape(1), shape(2), shape(4)],
-        in_specs=specs(pltpu.VMEM, 5),
-        out_specs=specs(pltpu.VMEM, 3),
+        out_shape=[jax.ShapeDtypeStruct((n * 3, feats, BINS), F32) for n in (1, 2, 4)],
+        in_specs=specs(pltpu.VMEM, 7),
+        out_specs=specs(pltpu.HBM, 3),
         scratch_shapes=[
-            pltpu.VMEM((owners * feats, cap), F32),
-            pltpu.VMEM((owners * feats, cap), F32),
             pltpu.VMEM((HI * 12, owners * cap), BF),
             pltpu.VMEM((12 * feats, BINS // 2), F32),
             pltpu.VMEM((12 * feats, BINS // 2), F32),
+            pltpu.VMEM((3, feats, BINS), F32),
+            pltpu.VMEM((6, feats, BINS), F32),
+            pltpu.VMEM((12, feats, BINS), F32),
+            pltpu.SemaphoreType.DMA((feats // FINISH, 3)),
         ],
         compiler_params=params,
         name="hist",
-    )(got, own, *others)
+    )(got, hi, lo, own, *others)
     return (
         node_moments.reshape(1, 3, feats, BINS),
         child_moments.reshape(2, 3, feats, BINS),

time: 48.4 us -> 44.3 us (0.915)
  Pallas kernels: 17.7 us -> 14.5 us
  local copies, waits for them, and re-layouts: 0.67 us -> 0 us
    pallas_call x1 -> x2, Pallas kernels: 13.9 us -> 11.1 us  [the longest x1 10.9 us: on_device(): pl.pallas_call(hist_kernel, out_shape=[jax.ShapeDtypeStruct((n * 3, feats...]
    unnamed x8 -> x0, local copies, waits for them, and re-layouts: 0.67 us -> none
where the time goes in v3:
time: 44.3 us; the launch traced here: 44.1 us
  blocking collectives  21.5 us (49%)
  Pallas kernels  14.5 us (33%)
  starting transfers between devices  3.84 us (9%)
  waiting for transfers between devices  3.6 us (8%)
  between operations  0.66 us (1%)
    all_to_all x1, blocking collectives, on_device(): got = lax.all_to_all(buf, 'rows', 0, 0, tiled=True)  21.5 us
    pallas_call x1, Pallas kernels, on_device(): pl.pallas_call(hist_kernel, out_shape=[jax.ShapeDtypeStruct((n * 3, feats...  10.9 us
    ppermute x3, starting transfers between devices, on_device(): lax.ppermute(own, 'feat', [(i, (i + k) % feat_devices) for i in range(fea...  3.84 us
    ppermute x3, waiting for transfers between devices, on_device(): lax.ppermute(own, 'feat', [(i, (i + k) % feat_devices) for i in range(fea...  3.6 us
    pallas_call x1, Pallas kernels, on_device(): pl.pallas_call(place_kernel, out_shape=[jax.ShapeDtypeStruct((nodes, dept...  2.83 us
  transfers between devices with their start and end apart: 3, of which 2 were waited for; matrix products, arithmetic and copies ran while one was open for 0% of the time, Pallas kernels for 0%

profile of v3, /device:TPU:1, one launch (start us, length us, event | category | flops | bytes accessed | tf_op | source)
XLA Modules:
  0.0 44.1 jit_solution(17067300668086355247)
XLA Ops:
  0.6 2.8 %place.1 = (bf16[32,72,128]{2,1,0:T(8,128)(2,1)S(1)}, s32[8,128]{1,0:T(8,128)S(1)}) custom-call(s32[1]{0:T(128)} %bitcast.owner_ref, s32[1]{0:T(128)} %bitcast.1.place_ref, s32[1,2048]{1,0:T(1,128)} %bitcast.11, f32[1,2048]{1,0:T(1,128)} %bitcast.12, f32[1,2048]{1,0:T(1,128)} %bitcast.13, f32[1,2048]{1,0:T(1,128)} %bitcast.14, s32[64,2048]{1,0:T(8,128)} %bitcast.10, ...), custom_call_target="tpu_custom_call" | custom-call | tf_op jit(solution)/shard_map/place/pallas_call | solution.py:222
  3.5 21.5 %all_to_all.5.got_ref = bf16[32,72,128]{2,1,0:T(8,128)(2,1)S(1)} all-to-all(bf16[32,72,128]{2,1,0:T(8,128)(2,1)S(1)} %get-tuple-element.10), channel_id=1, replica_groups=mesh['rows'=32,'feat'=4] {'rows'}, dimensions={0} | all-to-all | bytes 1179648 | tf_op jit(solution)/shard_map/all_to_all | solution.py:249
  25.0 0.5 %split.1.b0_ref = bf16[3,32,128]{2,1,0:T(8,128)(2,1)S(1)} custom-call(s32[8,128]{1,0:T(8,128)S(1)} %get-tuple-element.13.split_ref, bf16[32,72,128]{2,1,0:T(8,128)(2,1)S(1)} %all_to_all.5.got_ref), custom_call_target="tpu_custom_call" | custom-call | tf_op jit(solution)/shard_map/split/pallas_call | solution.py:250
  25.5 2.8 %collective-permute-start.2 = (bf16[3,32,128]{2,1,0:T(8,128)(2,1)S(1)}, bf16[3,32,128]{2,1,0:T(8,128)(2,1)S(1)}, u32[]{:S(2)}, u32[]{:S(2)}) collective-permute-start(bf16[3,32,128]{2,1,0:T(8,128)(2,1)S(1)} %split.1.b0_ref), channel_id=1, source_target_pairs={{0,3},{1,0},{2,1},{3,2},{4,7},{5,4},{6,5},{7,6},{8,11},{9,8},{10,9... | collective-permute-start | bytes 73736 | tf_op jit(solution)/shard_map/ppermute | solution.py:259
  28.3 0.4 collective-permute-start.1
  28.7 0.7 %collective-permute-start = (bf16[3,32,128]{2,1,0:T(8,128)(2,1)S(1)}, bf16[3,32,128]{2,1,0:T(8,128)(2,1)S(1)}, u32[]{:S(2)}, u32[]{:S(2)}) collective-permute-start(bf16[3,32,128]{2,1,0:T(8,128)(2,1)S(1)} %split.1.b0_ref), channel_id=1, source_target_pairs={{0,1},{1,2},{2,3},{3,0},{4,5},{5,6},{6,7},{7,4},{8,9},{9,10},{10,1... | collective-permute-start | bytes 73736 | tf_op jit(solution)/shard_map/ppermute | solution.py:259
  29.4 0.2 prepare.1
  29.5 0.0 collective-permute-done.2.b3_ref
  29.6 3.0 %collective-permute-done.1.b2_ref = bf16[3,32,128]{2,1,0:T(8,128)(2,1)S(1)} collective-permute-done((bf16[3,32,128]{2,1,0:T(8,128)(2,1)S(1)}, bf16[3,32,128]{2,1,0:T(8,128)(2,1)S(1)}, u32[]{:S(2)}, u32[]{:S(2)}) %collective-permute-start.1) | collective-permute-done | bytes 24608 | tf_op jit(solution)/shard_map/ppermute | solution.py:259
  32.5 0.6 %collective-permute-done.b1_ref = bf16[3,32,128]{2,1,0:T(8,128)(2,1)S(1)} collective-permute-done((bf16[3,32,128]{2,1,0:T(8,128)(2,1)S(1)}, bf16[3,32,128]{2,1,0:T(8,128)(2,1)S(1)}, u32[]{:S(2)}, u32[]{:S(2)}) %collective-permute-start) | collective-permute-done | bytes 24608 | tf_op jit(solution)/shard_map/ppermute | solution.py:259
  33.2 10.9 %hist.1 = (f32[3,64,256]{2,1,0:T(8,128)}, f32[6,64,256]{2,1,0:T(8,128)}, f32[12,64,256]{2,1,0:T(8,128)}) custom-call(bf16[32,72,128]{2,1,0:T(8,128)(2,1)S(1)} %all_to_all.5.got_ref, f32[2048,128]{1,0:T(8,128)S(1)} %get-tuple-element.11.hi_ref, f32[2048,128]{1,0:T(8,128)S(1)} %get-tuple-element.12.lo_ref, bf16[3,32,128]{2,1,0:T(8,128)(2,1)S(1)} %split.1.b0_ref, ...), custom_call_target="tpu_custom_call" | custom-call | tf_op jit(solution)/shard_map/hist/pallas_call | solution.py:271
Async XLA Ops:
  25.5 4.0 %collective-permute-start.2 = (bf16[3,32,128]{2,1,0:T(8,128)(2,1)S(1)}, bf16[3,32,128]{2,1,0:T(8,128)(2,1)S(1)}, u32[]{:S(2)}, u32[]{:S(2)}) collective-permute-start(bf16[3,32,128]{2,1,0:T(8,128)(2,1)S(1)} %split.1.b0_ref), channel_id=1, source_target_pairs={{0,3},{1,0},{2,1},{3,2},{4,7},{5,4},{6,5},{7,6},{8,11},{9,8},{10,9... | collective-permute-start | bytes 73736 | tf_op jit(solution)/shard_map/ppermute | solution.py:259
  28.3 4.2 %collective-permute-start.1 = (bf16[3,32,128]{2,1,0:T(8,128)(2,1)S(1)}, bf16[3,32,128]{2,1,0:T(8,128)(2,1)S(1)}, u32[]{:S(2)}, u32[]{:S(2)}) collective-permute-start(bf16[3,32,128]{2,1,0:T(8,128)(2,1)S(1)} %split.1.b0_ref), channel_id=1, source_target_pairs={{0,2},{1,3},{2,0},{3,1},{4,6},{5,7},{6,4},{7,5},{8,10},{9,11},{10,... | collective-permute-start | bytes 73736 | tf_op jit(solution)/shard_map/ppermute | solution.py:259
  28.7 4.5 %collective-permute-start = (bf16[3,32,128]{2,1,0:T(8,128)(2,1)S(1)}, bf16[3,32,128]{2,1,0:T(8,128)(2,1)S(1)}, u32[]{:S(2)}, u32[]{:S(2)}) collective-permute-start(bf16[3,32,128]{2,1,0:T(8,128)(2,1)S(1)} %split.1.b0_ref), channel_id=1, source_target_pairs={{0,1},{1,2},{2,3},{3,0},{4,5},{5,6},{6,7},{7,4},{8,9},{9,10},{10,1... | collective-permute-start | bytes 73736 | tf_op jit(solution)/shard_map/ppermute | solution.py:259

commit v4 on v3

--- a/solution.py
+++ b/solution.py
@@ -20,23 +20,56 @@
     return lax.broadcasted_iota(jnp.int32, shape, axis)
 
 
-def place_kernel(
-    owner_ref, place_ref, node_hbm, w_hbm, t_hbm, y_hbm, bins_hbm, rf_hbm, cf_hbm, rc_hbm, cc_hbm,
-    out_ref, split_ref, node_ref, w_ref, t_ref, y_ref, bins_ref, rf_ref, cf_ref, rc_ref, cc_ref,
-    a_ref, sems,
-):
-    copies = [
-        pltpu.make_async_copy(source, target, sems.at[i])
-        for i, (source, target) in enumerate(
-            (
-                (node_hbm, node_ref), (w_hbm, w_ref), (t_hbm, t_ref), (y_hbm, y_ref),
-                (bins_hbm, bins_ref), (rf_hbm, rf_ref), (cf_hbm, cf_ref), (rc_hbm, rc_ref),
-                (cc_hbm, cc_ref),
-            )
-        )
-    ]
+def start_all(pairs, sems):
+    copies = [pltpu.make_async_copy(pair[0], pair[1], sems.at[i]) for i, pair in enumerate(pairs)]
     for copy in copies:
         copy.start()
+    return copies
+
+
+def decide_kernel(
+    place_ref, node_hbm, bins_hbm, rf_hbm, rc_hbm, cf_hbm, cc_hbm, bits_ref, out_ref, node_ref,
+    bins_ref, rf_ref, rc_ref, cf_ref, cc_ref, sems,
+):
+    copies = start_all(
+        (
+            (node_hbm, node_ref), (rf_hbm, rf_ref), (rc_hbm, rc_ref), (cf_hbm, cf_ref),
+            (cc_hbm, cc_ref), (bins_hbm, bins_ref),
+        ),
+        sems,
+    )
+    feats, rows = bins_ref.shape
+    nodes = rf_ref.shape[1]
+    first = place_ref[0] * feats
+    for copy in copies[:5]:
+        copy.wait()
+    node = node_ref[...]
+
+    def look_up(feature_row, cutoff_row, index, count):
+        here = (feature_row - first == iota((feats, count), 0)).astype(F32)
+        table = jnp.concatenate([here, jnp.broadcast_to(cutoff_row.astype(F32), (8, count))], 0)
+        hot = (iota((count, rows), 0) == index).astype(F32).astype(BF)
+        return lax.dot_general(table.astype(BF), hot, NN, preferred_element_type=F32)
+
+    got = [
+        look_up(rf_ref[...], rc_ref[...], node, nodes),
+        look_up(cf_ref[...], cc_ref[...], 2 * node, 2 * nodes),
+        look_up(cf_ref[...], cc_ref[...], 2 * node + 1, 2 * nodes),
+    ]
+    copies[5].wait()
+    bins = bins_ref[...].astype(F32)
+    out_ref[...] = bins.astype(BF)
+    bits = [
+        jnp.sum(jnp.where(bins > g[feats : feats + 1], g[:feats], 0.0), 0, keepdims=True) for g in got
+    ]
+    bits_ref[...] = jnp.concatenate(bits + [jnp.zeros((5, rows), F32)], 0).astype(BF)
+
+
+def place_kernel(
+    bins_ref, node_hbm, w_hbm, t_hbm, y_hbm, out_ref, value_ref, node_ref, w_ref, t_ref, y_ref, a_ref,
+    sems,
+):
+    copies = start_all(((node_hbm, node_ref), (w_hbm, w_ref), (t_hbm, t_ref), (y_hbm, y_ref)), sems)
     feats, rows = bins_ref.shape
     nodes, depth, cap = out_ref.shape
     blocks = rows // 256
@@ -57,48 +90,51 @@
     rank = jnp.concatenate(ranks, 1)
     code = rank.astype(jnp.int32) + node % 2 * cap
     slot_hot = (iota((2 * cap, rows), 0) == code).astype(F32).astype(BF)
-    for copy in copies[1:4]:
+    bins = bins_ref[...]
+    pair = jnp.broadcast_to(node // 2, (feats, rows))
+    for p in range(nodes // 2):
+        a_ref[p * feats : (p + 1) * feats, :] = jnp.where(pair == p, bins, jnp.zeros((), BF))
+    moved = lax.dot_general(a_ref[...], slot_hot, NT, preferred_element_type=F32).astype(BF)
+    for p in range(nodes // 2):
+        piece = moved[p * feats : (p + 1) * feats]
+        out_ref[2 * p, :feats, :] = piece[:, :cap]
+        out_ref[2 * p + 1, :feats, :] = piece[:, cap:]
+    for copy in copies[1:]:
         copy.wait()
     w = w_ref[...]
     t = t_ref[...]
     y = y_ref[...]
-    carried = jnp.concatenate([w, w * t * t, w * t * y, jnp.zeros((depth - feats - 3, rows), F32)], 0)
-    copies[4].wait()
-    bins = jnp.concatenate([bins_ref[...].astype(F32), carried], 0).astype(BF)
-    pair = jnp.broadcast_to(node // 2, (depth, rows))
+    value_ref[...] = jnp.concatenate(
+        [w, w * t * t, w * t * y, code.astype(F32), (node // 2).astype(F32), jnp.zeros((3, rows), F32)], 0
+    )
+
+
+def value_kernel(bits_ref, other_ref, value_ref, buf_ref, out_ref, part_ref, sem):
+    nodes, _, cap = part_ref.shape
+    rows = value_ref.shape[1]
+    bits = bits_ref[...].astype(F32) + other_ref[...].astype(F32)
+    carried = jnp.concatenate([value_ref[:3, :], bits[:5]], 0)
+    code = value_ref[3:4, :].astype(jnp.int32)
+    slot_hot = (iota((2 * cap, rows), 0) == code).astype(F32).astype(BF)
+    pair = jnp.broadcast_to(value_ref[4:5, :], (8, rows))
+    spread = jnp.concatenate(
+        [jnp.where(pair == float(p), carried, 0.0) for p in range(nodes // 2)], 0
+    ).astype(BF)
+    moved = lax.dot_general(spread, slot_hot, NT, preferred_element_type=F32).astype(BF)
     for p in range(nodes // 2):
-        a_ref[p * depth : (p + 1) * depth, :] = jnp.where(pair == p, bins, jnp.zeros((), BF))
-    moved = lax.dot_general(a_ref[...], slot_hot, NT, preferred_element_type=F32).astype(BF)
-    for p in range(nodes // 2):
-        piece = moved[p * depth : (p + 1) * depth]
-        out_ref[2 * p] = piece[:, :cap]
-        out_ref[2 * p + 1] = piece[:, cap:]
-    for copy in copies[5:]:
-        copy.wait()
-    own = owner_ref[0]
-    first = place_ref[0] * feats
-    table = [
-        rf_ref[own] - first, cf_ref[2 * own] - first, cf_ref[2 * own + 1] - first,
-        rc_ref[own], cc_ref[2 * own], cc_ref[2 * own + 1],
-    ]
-    for k, entry in enumerate(table):
-        split_ref[k : k + 1, :] = jnp.full((1, cap), entry, jnp.int32)
-
-
-def split_kernel(split_ref, got_ref, bits_ref):
-    sources, depth, cap = got_ref.shape
-    feats = depth - 8
-    feature = iota((feats, cap), 0)
-    masks = [feature == split_ref[k : k + 1, :] for k in range(3)]
-    cutoffs = [split_ref[k : k + 1, :].astype(F32) for k in range(3, 6)]
-    rows = [[], [], []]
-    for s in range(sources):
-        x = got_ref[s, :feats, :].astype(F32)
-        for k in range(3):
-            right = jnp.where(jnp.logical_and(masks[k], x > cutoffs[k]), 1.0, 0.0)
-            rows[k].append(jnp.sum(right, 0, keepdims=True))
+        piece = moved[p * 8 : (p + 1) * 8]
+        part_ref[2 * p] = piece[:, :cap]
+        part_ref[2 * p + 1] = piece[:, cap:]
+    copy = pltpu.make_async_copy(part_ref, out_ref.at[:, pl.ds(out_ref.shape[1] - 8, 8), :], sem)
+    copy.start()
+    copy.wait()
+
+
+def tail_kernel(got_ref, bits_ref):
+    sources, depth, _ = got_ref.shape
+    tails = [got_ref[s, depth - 8 :, :].astype(F32) for s in range(sources)]
     for k in range(3):
-        bits_ref[k] = jnp.concatenate(rows[k], 0).astype(BF)
+        bits_ref[k] = jnp.concatenate([tail[3 + k : 4 + k] for tail in tails], 0).astype(BF)
 
 
 def prepare_kernel(got_ref, hi_ref, lo_ref):
@@ -112,16 +148,14 @@
 
 
 def hist_kernel(
-    got_ref, hi_ref, lo_ref, b0_ref, b1_ref, b2_ref, b3_ref, node_hbm, child_hbm, leaf_hbm, w_ref,
-    half0_ref, half1_ref, node_ref, child_ref, leaf_ref, sems,
+    got_ref, hi_ref, lo_ref, bits_ref, other_ref, node_hbm, child_hbm, leaf_hbm, w_ref, half0_ref,
+    half1_ref, node_ref, child_ref, leaf_ref, sems,
 ):
     sources, depth, cap = got_ref.shape
     feats = depth - 8
     cols = leaf_ref.shape[0]
     halves = (half0_ref, half1_ref)
-    bits = (b0_ref[...].astype(F32) + b1_ref[...].astype(F32)) + (
-        b2_ref[...].astype(F32) + b3_ref[...].astype(F32)
-    )
+    bits = bits_ref[...].astype(F32) + other_ref[...].astype(F32)
     leaf = 2.0 * bits[0] + jnp.where(bits[0] > 0.5, bits[2], bits[1])
     for s in range(sources):
         tail = got_ref[s, feats:, :].astype(F32)
@@ -214,51 +248,67 @@
     cap = 2 * rows // nodes
     depth = feats + 8
     params = pltpu.CompilerParams(vmem_limit_bytes=24 << 20)
-    here = lambda name: lax.axis_index(name).astype(jnp.int32)[None]
-    sources = [
-        node_index.T, unit_weight[None], treatment[None], outcome[None], binned.T,
-        root_feature, child_feature, root_cutoff, child_cutoff,
-    ]
-    buf, splits = pl.pallas_call(
+    in_hbm = lambda *xs: [pltpu.with_memory_space_constraint(x, pltpu.HBM) for x in xs]
+    row = lambda dtype: pltpu.VMEM((1, rows), dtype)
+    swap = lambda x, bit: lax.ppermute(x, "feat", [(i, i ^ bit) for i in range(feat_devices)])
+    bins, node = in_hbm(binned.T, node_index.T)
+    own, narrow = pl.pallas_call(
+        decide_kernel,
+        out_shape=[jax.ShapeDtypeStruct((8, rows), BF), jax.ShapeDtypeStruct((feats, rows), BF)],
+        in_specs=specs(pltpu.SMEM, 1) + specs(pltpu.HBM, 6),
+        out_specs=specs(pltpu.VMEM, 2),
+        scratch_shapes=[
+            row(jnp.int32),
+            pltpu.VMEM((feats, rows), jnp.int32),
+            pltpu.VMEM((1, nodes), jnp.int32),
+            pltpu.VMEM((1, nodes), jnp.int32),
+            pltpu.VMEM((1, 2 * nodes), jnp.int32),
+            pltpu.VMEM((1, 2 * nodes), jnp.int32),
+            pltpu.SemaphoreType.DMA((6,)),
+        ],
+        compiler_params=params,
+        name="decide",
+    )(
+        lax.axis_index("feat").astype(jnp.int32)[None], node, bins,
+        *in_hbm(root_feature[None], root_cutoff[None], child_feature[None], child_cutoff[None]),
+    )
+    other = swap(own, 1)
+    buf, value = pl.pallas_call(
         place_kernel,
         out_shape=[
             jax.ShapeDtypeStruct((nodes, depth, cap), BF),
-            jax.ShapeDtypeStruct((8, cap), jnp.int32),
+            jax.ShapeDtypeStruct((8, rows), F32),
         ],
-        in_specs=specs(pltpu.SMEM, 2) + specs(pltpu.HBM, 9),
+        in_specs=specs(pltpu.VMEM, 1) + specs(pltpu.HBM, 4),
         out_specs=specs(pltpu.VMEM, 2),
         scratch_shapes=[
-            pltpu.VMEM((1, rows), jnp.int32),
-            pltpu.VMEM((1, rows), F32),
-            pltpu.VMEM((1, rows), F32),
-            pltpu.VMEM((1, rows), F32),
-            pltpu.VMEM((feats, rows), jnp.int32),
-            pltpu.SMEM((nodes,), jnp.int32),
-            pltpu.SMEM((2 * nodes,), jnp.int32),
-            pltpu.SMEM((nodes,), jnp.int32),
-            pltpu.SMEM((2 * nodes,), jnp.int32),
-            pltpu.VMEM((nodes // 2 * depth, rows), BF),
-            pltpu.SemaphoreType.DMA((9,)),
+            row(jnp.int32), row(F32), row(F32), row(F32),
+            pltpu.VMEM((nodes // 2 * feats, rows), BF),
+            pltpu.SemaphoreType.DMA((4,)),
         ],
         compiler_params=params,
         name="place",
-    )(
-        here("rows"), here("feat"),
-        *[pltpu.with_memory_space_constraint(x, pltpu.HBM) for x in sources],
-    )
+    )(narrow, node, *in_hbm(unit_weight[None], treatment[None], outcome[None]))
+    buf = pl.pallas_call(
+        value_kernel,
+        out_shape=jax.ShapeDtypeStruct((nodes, depth, cap), BF),
+        in_specs=specs(pltpu.VMEM, 3) + specs(pl.ANY, 1),
+        out_specs=specs(pl.ANY, 1)[0],
+        scratch_shapes=[pltpu.VMEM((nodes, 8, cap), BF), pltpu.SemaphoreType.DMA],
+        input_output_aliases={3: 0},
+        compiler_params=params,
+        name="value",
+    )(own, other, value, buf)
     got = lax.all_to_all(buf, "rows", 0, 0, tiled=True)
-    own = pl.pallas_call(
-        split_kernel,
+    half = pl.pallas_call(
+        tail_kernel,
         out_shape=jax.ShapeDtypeStruct((3, owners, cap), BF),
-        in_specs=specs(pltpu.VMEM, 2),
+        in_specs=specs(pltpu.VMEM, 1),
         out_specs=specs(pltpu.VMEM, 1)[0],
         compiler_params=params,
-        name="split",
-    )(splits, got)
-    others = [
-        lax.ppermute(own, "feat", [(i, (i + k) % feat_devices) for i in range(feat_devices)])
-        for k in range(1, feat_devices)
-    ]
+        name="tail",
+    )(got)
+    rest = swap(half, 2)
     digit = jax.ShapeDtypeStruct((owners * feats, cap), F32)
     hi, lo = pl.pallas_call(
         prepare_kernel,
@@ -271,7 +321,7 @@
     node_moments, child_moments, leaf_moments = pl.pallas_call(
         hist_kernel,
         out_shape=[jax.ShapeDtypeStruct((n * 3, feats, BINS), F32) for n in (1, 2, 4)],
-        in_specs=specs(pltpu.VMEM, 7),
+        in_specs=specs(pltpu.VMEM, 5),
         out_specs=specs(pltpu.HBM, 3),
         scratch_shapes=[
             pltpu.VMEM((HI * 12, owners * cap), BF),
@@ -284,7 +334,7 @@
         ],
         compiler_params=params,
         name="hist",
-    )(got, hi, lo, own, *others)
+    )(got, hi, lo, half, rest)
     return (
         node_moments.reshape(1, 3, feats, BINS),
         child_moments.reshape(2, 3, feats, BINS),

time: 44.3 us -> 44 us (level)
  waiting for transfers between devices: 3.6 us -> 1.47 us
  starting transfers between devices: 3.84 us -> 5.15 us
  Pallas kernels: 14.5 us -> 15.4 us
  blocking collectives: 21.5 us -> 21 us
    ppermute x3 -> x2, waiting for transfers between devices: 3.6 us -> 1.47 us  [on_device(): lax.ppermute(x, 'feat', [(i, i ^ bit) for i in range(feat_devices)])]
    pallas_call x1 -> x3, Pallas kernels: 0.53 us -> 1.98 us  [the longest x1 1.43 us: on_device(): pl.pallas_call(decide_kernel, out_shape=[jax.ShapeDtypeStruct((8, rows),...]
    ppermute x3 -> x2, starting transfers between devices: 3.84 us -> 5.15 us  [on_device(): lax.ppermute(x, 'feat', [(i, i ^ bit) for i in range(feat_devices)])]
    all_to_all x1, blocking collectives: 21.5 us -> 21 us  [on_device(): got = lax.all_to_all(buf, 'rows', 0, 0, tiled=True)]
    pallas_call x1, Pallas kernels: 2.83 us -> 2.37 us  [on_device(): pl.pallas_call(place_kernel, out_shape=[jax.ShapeDtypeStruct((nodes, dept...]
  transfers between devices with their start and end apart: 3 -> 2, of which waited for: 2 -> 1; matrix products, arithmetic and copies ran while one was open for 0% -> 0% of each run, Pallas kernels for 0% -> 6%
where the time goes in v4:
time: 44 us; the launch traced here: 43.7 us
  blocking collectives  21 us (48%)
  Pallas kernels  15.4 us (35%)
  starting transfers between devices  5.15 us (12%)
  waiting for transfers between devices  1.47 us (3%)
  between operations  0.68 us (2%)
    all_to_all x1, blocking collectives, on_device(): got = lax.all_to_all(buf, 'rows', 0, 0, tiled=True)  21 us
    pallas_call x1, Pallas kernels, on_device(): pl.pallas_call(hist_kernel, out_shape=[jax.ShapeDtypeStruct((n * 3, feats...  10.9 us
    ppermute x2, starting transfers between devices, on_device(): lax.ppermute(x, 'feat', [(i, i ^ bit) for i in range(feat_devices)])  5.15 us
    pallas_call x1, Pallas kernels, on_device(): pl.pallas_call(place_kernel, out_shape=[jax.ShapeDtypeStruct((nodes, dept...  2.37 us
    ppermute x2, waiting for transfers between devices, on_device(): lax.ppermute(x, 'feat', [(i, i ^ bit) for i in range(feat_devices)])  1.47 us
    pallas_call x1, Pallas kernels, on_device(): pl.pallas_call(decide_kernel, out_shape=[jax.ShapeDtypeStruct((8, rows),...  1.43 us
  transfers between devices with their start and end apart: 2, of which 1 were waited for; matrix products, arithmetic and copies ran while one was open for 0% of the time, Pallas kernels for 6%

profile of v4, /device:TPU:1, one launch (start us, length us, event | category | flops | bytes accessed | tf_op | source)
XLA Modules:
  0.0 43.7 jit_solution(18172087207550051731)
XLA Ops:
  0.6 1.4 %decide.1 = (bf16[8,2048]{1,0:T(8,128)(2,1)S(1)}, bf16[64,2048]{1,0:T(8,128)(2,1)S(1)}) custom-call(s32[1]{0:T(128)} %bitcast.place_ref, s32[1,2048]{1,0:T(1,128)} %bitcast.14, s32[64,2048]{1,0:T(8,128)} %bitcast.13, s32[1,32]{1,0:T(1,128)} %bitcast.19, s32[1,32]{1,0:T(1,128)} %bitcast.20, s32[1,64]{1,0:T(1,128)} %bitcast.21, s32[1,64]{1,0:T(1,128)} %bitcast.22), custom_call_target="tpu_custom_call" | custom-call | tf_op jit(solution)/shard_map/decide/pallas_call | solution.py:255
  2.1 2.2 %collective-permute-start = (bf16[8,2048]{1,0:T(8,128)(2,1)S(1)}, bf16[8,2048]{1,0:T(8,128)(2,1)S(1)}, u32[]{:S(2)}, u32[]{:S(2)}) collective-permute-start(bf16[8,2048]{1,0:T(8,128)(2,1)S(1)} %get-tuple-element.12.bits_ref), channel_id=1, source_target_pairs={{0,1},{1,0},{2,3},{3,2},{4,5},{5,4},{6,7},{7,6},{8,9},{9,8},{10,11... | collective-permute-start | bytes 98312 | tf_op jit(solution)/shard_map/ppermute | solution.py:253
  4.3 2.4 %place.1 = (bf16[32,72,128]{2,1,0:T(8,128)(2,1)S(1)}, f32[8,2048]{1,0:T(8,128)S(1)}) custom-call(bf16[64,2048]{1,0:T(8,128)(2,1)S(1)} %get-tuple-element.13.bins_ref, s32[1,2048]{1,0:T(1,128)} %bitcast.15, f32[1,2048]{1,0:T(1,128)} %bitcast.16, f32[1,2048]{1,0:T(1,128)} %bitcast.17, f32[1,2048]{1,0:T(1,128)} %bitcast.18), custom_call_target="tpu_custom_call" | custom-call | tf_op jit(solution)/shard_map/place/pallas_call | solution.py:276
  6.7 0.0 collective-permute-done.other_ref
  6.7 0.5 %value.1 = bf16[32,72,128]{2,1,0:T(8,128)(2,1)S(1)} custom-call(bf16[8,2048]{1,0:T(8,128)(2,1)S(1)} %get-tuple-element.12.bits_ref, bf16[8,2048]{1,0:T(8,128)(2,1)S(1)} %collective-permute-done.other_ref, f32[8,2048]{1,0:T(8,128)S(1)} %get-tuple-element.14.value_ref, bf16[32,72,128]{2,1,0:T(8,128)(2,1)S(1)} %get-tuple-element.15.buf_ref), custom_call_target="tpu_custom_call", output_to_operand_aliasing={{}: (3, {})} | custom-call | tf_op jit(solution)/shard_map/value/pallas_call | solution.py:292
  7.2 21.0 %all_to_all.5.got_ref = bf16[32,72,128]{2,1,0:T(8,128)(2,1)S(1)} all-to-all(bf16[32,72,128]{2,1,0:T(8,128)(2,1)S(1)} %value.1), channel_id=1, replica_groups=mesh['rows'=32,'feat'=4] {'rows'}, dimensions={0} | all-to-all | bytes 1179648 | tf_op jit(solution)/shard_map/all_to_all | solution.py:302
  28.2 2.9 %collective-permute-start.1 = (bf16[3,32,128]{2,1,0:T(8,128)(2,1)S(1)}, bf16[3,32,128]{2,1,0:T(8,128)(2,1)S(1)}, u32[]{:S(2)}, u32[]{:S(2)}) collective-permute-start(bf16[3,32,128]{2,1,0:T(8,128)(2,1)S(1)} %tail.1.bits_ref), channel_id=1, source_target_pairs={{0,2},{1,3},{2,0},{3,1},{4,6},{5,7},{6,4},{7,5},{8,10},{9,11},{10,... | collective-permute-start | bytes 73736 | tf_op jit(solution)/shard_map/ppermute | solution.py:253
  31.1 0.2 prepare.1
  31.3 1.5 %collective-permute-done.1.other_ref = bf16[3,32,128]{2,1,0:T(8,128)(2,1)S(1)} collective-permute-done((bf16[3,32,128]{2,1,0:T(8,128)(2,1)S(1)}, bf16[3,32,128]{2,1,0:T(8,128)(2,1)S(1)}, u32[]{:S(2)}, u32[]{:S(2)}) %collective-permute-start.1) | collective-permute-done | bytes 24608 | tf_op jit(solution)/shard_map/ppermute | solution.py:253
  32.8 10.9 %hist.1 = (f32[3,64,256]{2,1,0:T(8,128)}, f32[6,64,256]{2,1,0:T(8,128)}, f32[12,64,256]{2,1,0:T(8,128)}) custom-call(bf16[32,72,128]{2,1,0:T(8,128)(2,1)S(1)} %all_to_all.5.got_ref, f32[2048,128]{1,0:T(8,128)S(1)} %get-tuple-element.16.hi_ref, f32[2048,128]{1,0:T(8,128)S(1)} %get-tuple-element.17.lo_ref, bf16[3,32,128]{2,1,0:T(8,128)(2,1)S(1)} %tail.1.bits_ref, ...), custom_call_target="tpu_custom_call" | custom-call | tf_op jit(solution)/shard_map/hist/pallas_call | solution.py:321
  (1 shorter events, 0.0 us)
Async XLA Ops:
  2.1 4.6 %collective-permute-start = (bf16[8,2048]{1,0:T(8,128)(2,1)S(1)}, bf16[8,2048]{1,0:T(8,128)(2,1)S(1)}, u32[]{:S(2)}, u32[]{:S(2)}) collective-permute-start(bf16[8,2048]{1,0:T(8,128)(2,1)S(1)} %get-tuple-element.12.bits_ref), channel_id=1, source_target_pairs={{0,1},{1,0},{2,3},{3,2},{4,5},{5,4},{6,7},{7,6},{8,9},{9,8},{10,11... | collective-permute-start | bytes 98312 | tf_op jit(solution)/shard_map/ppermute | solution.py:253
  28.2 4.6 %collective-permute-start.1 = (bf16[3,32,128]{2,1,0:T(8,128)(2,1)S(1)}, bf16[3,32,128]{2,1,0:T(8,128)(2,1)S(1)}, u32[]{:S(2)}, u32[]{:S(2)}) collective-permute-start(bf16[3,32,128]{2,1,0:T(8,128)(2,1)S(1)} %tail.1.bits_ref), channel_id=1, source_target_pairs={{0,2},{1,3},{2,0},{3,1},{4,6},{5,7},{6,4},{7,5},{8,10},{9,11},{10,... | collective-permute-start | bytes 73736 | tf_op jit(solution)/shard_map/ppermute | solution.py:253

commit v5 on v4

--- a/solution.py
+++ b/solution.py
@@ -12,7 +12,7 @@
 NN = (((1,), (0,)), ((), ()))
 HI = 4
 LO = BINS // HI
-UNROLL = 16
+UNROLL = 32
 FINISH = 32
 
 
@@ -308,7 +308,7 @@
         compiler_params=params,
         name="tail",
     )(got)
-    rest = swap(half, 2)
+    rest = swap(half, 3)
     digit = jax.ShapeDtypeStruct((owners * feats, cap), F32)
     hi, lo = pl.pallas_call(
         prepare_kernel,

time: 44 us -> 43.3 us (0.984)
  no operation moved by 1% of the time
where the time goes in v5:
time: 43.3 us; the launch traced here: 43 us
  blocking collectives  21 us (48%)
  Pallas kernels  15 us (35%)
  starting transfers between devices  4.97 us (11%)
  waiting for transfers between devices  1.39 us (3%)
  between operations  0.68 us (2%)
    all_to_all x1, blocking collectives, on_device(): got = lax.all_to_all(buf, 'rows', 0, 0, tiled=True)  21 us
    pallas_call x1, Pallas kernels, on_device(): pl.pallas_call(hist_kernel, out_shape=[jax.ShapeDtypeStruct((n * 3, feats...  10.5 us
    ppermute x2, starting transfers between devices, on_device(): lax.ppermute(x, 'feat', [(i, i ^ bit) for i in range(feat_devices)])  4.97 us
    pallas_call x1, Pallas kernels, on_device(): pl.pallas_call(place_kernel, out_shape=[jax.ShapeDtypeStruct((nodes, dept...  2.37 us
    pallas_call x1, Pallas kernels, on_device(): pl.pallas_call(decide_kernel, out_shape=[jax.ShapeDtypeStruct((8, rows),...  1.43 us
    ppermute x2, waiting for transfers between devices, on_device(): lax.ppermute(x, 'feat', [(i, i ^ bit) for i in range(feat_devices)])  1.39 us
  transfers between devices with their start and end apart: 2, of which 1 were waited for; matrix products, arithmetic and copies ran while one was open for 0% of the time, Pallas kernels for 6%

profile of v5, /device:TPU:1, one launch (start us, length us, event | category | flops | bytes accessed | tf_op | source)
XLA Modules:
  0.0 43.0 jit_solution(16152833672765438570)
XLA Ops:
  0.6 1.4 %decide.1 = (bf16[8,2048]{1,0:T(8,128)(2,1)S(1)}, bf16[64,2048]{1,0:T(8,128)(2,1)S(1)}) custom-call(s32[1]{0:T(128)} %bitcast.place_ref, s32[1,2048]{1,0:T(1,128)} %bitcast.14, s32[64,2048]{1,0:T(8,128)} %bitcast.13, s32[1,32]{1,0:T(1,128)} %bitcast.19, s32[1,32]{1,0:T(1,128)} %bitcast.20, s32[1,64]{1,0:T(1,128)} %bitcast.21, s32[1,64]{1,0:T(1,128)} %bitcast.22), custom_call_target="tpu_custom_call" | custom-call | tf_op jit(solution)/shard_map/decide/pallas_call | solution.py:255
  2.1 2.2 %collective-permute-start = (bf16[8,2048]{1,0:T(8,128)(2,1)S(1)}, bf16[8,2048]{1,0:T(8,128)(2,1)S(1)}, u32[]{:S(2)}, u32[]{:S(2)}) collective-permute-start(bf16[8,2048]{1,0:T(8,128)(2,1)S(1)} %get-tuple-element.12.bits_ref), channel_id=1, source_target_pairs={{0,1},{1,0},{2,3},{3,2},{4,5},{5,4},{6,7},{7,6},{8,9},{9,8},{10,11... | collective-permute-start | bytes 98312 | tf_op jit(solution)/shard_map/ppermute | solution.py:253
  4.3 2.4 %place.1 = (bf16[32,72,128]{2,1,0:T(8,128)(2,1)S(1)}, f32[8,2048]{1,0:T(8,128)S(1)}) custom-call(bf16[64,2048]{1,0:T(8,128)(2,1)S(1)} %get-tuple-element.13.bins_ref, s32[1,2048]{1,0:T(1,128)} %bitcast.15, f32[1,2048]{1,0:T(1,128)} %bitcast.16, f32[1,2048]{1,0:T(1,128)} %bitcast.17, f32[1,2048]{1,0:T(1,128)} %bitcast.18), custom_call_target="tpu_custom_call" | custom-call | tf_op jit(solution)/shard_map/place/pallas_call | solution.py:276
  6.7 0.0 collective-permute-done.other_ref
  6.7 0.5 %value.1 = bf16[32,72,128]{2,1,0:T(8,128)(2,1)S(1)} custom-call(bf16[8,2048]{1,0:T(8,128)(2,1)S(1)} %get-tuple-element.12.bits_ref, bf16[8,2048]{1,0:T(8,128)(2,1)S(1)} %collective-permute-done.other_ref, f32[8,2048]{1,0:T(8,128)S(1)} %get-tuple-element.14.value_ref, bf16[32,72,128]{2,1,0:T(8,128)(2,1)S(1)} %get-tuple-element.15.buf_ref), custom_call_target="tpu_custom_call", output_to_operand_aliasing={{}: (3, {})} | custom-call | tf_op jit(solution)/shard_map/value/pallas_call | solution.py:292
  7.2 21.0 %all_to_all.5.got_ref = bf16[32,72,128]{2,1,0:T(8,128)(2,1)S(1)} all-to-all(bf16[32,72,128]{2,1,0:T(8,128)(2,1)S(1)} %value.1), channel_id=1, replica_groups=mesh['rows'=32,'feat'=4] {'rows'}, dimensions={0} | all-to-all | bytes 1179648 | tf_op jit(solution)/shard_map/all_to_all | solution.py:302
  28.2 2.8 %collective-permute-start.1 = (bf16[3,32,128]{2,1,0:T(8,128)(2,1)S(1)}, bf16[3,32,128]{2,1,0:T(8,128)(2,1)S(1)}, u32[]{:S(2)}, u32[]{:S(2)}) collective-permute-start(bf16[3,32,128]{2,1,0:T(8,128)(2,1)S(1)} %tail.1.bits_ref), channel_id=1, source_target_pairs={{0,3},{1,2},{2,1},{3,0},{4,7},{5,6},{6,5},{7,4},{8,11},{9,10},{10,... | collective-permute-start | bytes 73736 | tf_op jit(solution)/shard_map/ppermute | solution.py:253
  31.0 0.2 prepare.1
  31.1 1.4 %collective-permute-done.1.other_ref = bf16[3,32,128]{2,1,0:T(8,128)(2,1)S(1)} collective-permute-done((bf16[3,32,128]{2,1,0:T(8,128)(2,1)S(1)}, bf16[3,32,128]{2,1,0:T(8,128)(2,1)S(1)}, u32[]{:S(2)}, u32[]{:S(2)}) %collective-permute-start.1) | collective-permute-done | bytes 24608 | tf_op jit(solution)/shard_map/ppermute | solution.py:253
  32.5 10.5 %hist.1 = (f32[3,64,256]{2,1,0:T(8,128)}, f32[6,64,256]{2,1,0:T(8,128)}, f32[12,64,256]{2,1,0:T(8,128)}) custom-call(bf16[32,72,128]{2,1,0:T(8,128)(2,1)S(1)} %all_to_all.5.got_ref, f32[2048,128]{1,0:T(8,128)S(1)} %get-tuple-element.16.hi_ref, f32[2048,128]{1,0:T(8,128)S(1)} %get-tuple-element.17.lo_ref, bf16[3,32,128]{2,1,0:T(8,128)(2,1)S(1)} %tail.1.bits_ref, ...), custom_call_target="tpu_custom_call" | custom-call | tf_op jit(solution)/shard_map/hist/pallas_call | solution.py:321
  (1 shorter events, 0.0 us)
Async XLA Ops:
  2.1 4.6 %collective-permute-start = (bf16[8,2048]{1,0:T(8,128)(2,1)S(1)}, bf16[8,2048]{1,0:T(8,128)(2,1)S(1)}, u32[]{:S(2)}, u32[]{:S(2)}) collective-permute-start(bf16[8,2048]{1,0:T(8,128)(2,1)S(1)} %get-tuple-element.12.bits_ref), channel_id=1, source_target_pairs={{0,1},{1,0},{2,3},{3,2},{4,5},{5,4},{6,7},{7,6},{8,9},{9,8},{10,11... | collective-permute-start | bytes 98312 | tf_op jit(solution)/shard_map/ppermute | solution.py:253
  28.2 4.3 %collective-permute-start.1 = (bf16[3,32,128]{2,1,0:T(8,128)(2,1)S(1)}, bf16[3,32,128]{2,1,0:T(8,128)(2,1)S(1)}, u32[]{:S(2)}, u32[]{:S(2)}) collective-permute-start(bf16[3,32,128]{2,1,0:T(8,128)(2,1)S(1)} %tail.1.bits_ref), channel_id=1, source_target_pairs={{0,3},{1,2},{2,1},{3,0},{4,7},{5,6},{6,5},{7,4},{8,11},{9,10},{10,... | collective-permute-start | bytes 73736 | tf_op jit(solution)/shard_map/ppermute | solution.py:253

commit v6 on v5

--- a/solution.py
+++ b/solution.py
@@ -12,8 +12,7 @@
 NN = (((1,), (0,)), ((), ()))
 HI = 4
 LO = BINS // HI
-UNROLL = 32
-FINISH = 32
+FINISH = 16
 
 
 def iota(shape, axis):
@@ -137,39 +136,40 @@
         bits_ref[k] = jnp.concatenate([tail[3 + k : 4 + k] for tail in tails], 0).astype(BF)
 
 
-def prepare_kernel(got_ref, hi_ref, lo_ref):
-    sources, depth, _ = got_ref.shape
+def prepare_kernel(got_ref, hi_ref, lo_ref, moment_ref):
+    sources, depth, cap = got_ref.shape
     feats = depth - 8
+    which = iota((moment_ref.shape[0], cap), 0) % 3
     for s in range(sources):
         x = got_ref[s, :feats, :].astype(F32)
         hi = jnp.floor(x * (1.0 / LO))
         hi_ref[s * feats : (s + 1) * feats, :] = hi
         lo_ref[s * feats : (s + 1) * feats, :] = x - hi * LO
+        tail = got_ref[s, feats:, :].astype(F32)
+        moments = jnp.where(which == 0, tail[0:1], jnp.where(which == 1, tail[1:2], tail[2:3]))
+        moment_ref[:, s * cap : (s + 1) * cap] = moments.astype(BF)
 
 
 def hist_kernel(
-    got_ref, hi_ref, lo_ref, bits_ref, other_ref, node_hbm, child_hbm, leaf_hbm, w_ref, half0_ref,
+    hi_ref, lo_ref, moment_ref, bits_ref, other_ref, node_hbm, child_hbm, leaf_hbm, w_ref, half0_ref,
     half1_ref, node_ref, child_ref, leaf_ref, sems,
 ):
-    sources, depth, cap = got_ref.shape
-    feats = depth - 8
-    cols = leaf_ref.shape[0]
+    cols, feats, _ = leaf_ref.shape
+    _, sources, cap = bits_ref.shape
     halves = (half0_ref, half1_ref)
+    one = jnp.ones((), BF)
+    zero = jnp.zeros((), BF)
     bits = bits_ref[...].astype(F32) + other_ref[...].astype(F32)
     leaf = 2.0 * bits[0] + jnp.where(bits[0] > 0.5, bits[2], bits[1])
+    leaf_of = (iota((HI * cols, cap), 0) % cols // 3).astype(F32).astype(BF)
     for s in range(sources):
-        tail = got_ref[s, feats:, :].astype(F32)
-        position = jnp.broadcast_to(leaf[s : s + 1], (3, cap))
-        columns = jnp.concatenate(
-            [jnp.where(position == float(q), tail[:3], 0.0) for q in range(cols // 3)], 0
-        )
-        w_ref[:, s * cap : (s + 1) * cap] = jnp.concatenate([columns] * HI, 0).astype(BF)
+        at = slice(s * cap, (s + 1) * cap)
+        position = jnp.broadcast_to(leaf[s : s + 1], (HI * cols, cap)).astype(BF)
+        w_ref[:, at] = jnp.where(position == leaf_of, moment_ref[:, at], zero)
     hi_of = [((iota((16, cap), 0) + 16 * i) // cols).astype(F32).astype(BF) for i in range(HI * cols // 16)]
     lo_of = [(iota((16, cap), 0) + 16 * i).astype(F32).astype(BF) for i in range(LO // 16)]
-    one = jnp.ones((), BF)
-    zero = jnp.zeros((), BF)
-
-    def step(f, carry):
+
+    def step(f):
         res = None
         for k in range(sources // 2):
             a = []
@@ -191,7 +191,6 @@
         for half in range(2):
             parts = [res[h * cols : (h + 1) * cols] for h in (2 * half, 2 * half + 1)]
             halves[half][pl.ds(f, cols, stride=feats), :] = jnp.concatenate(parts, 1)
-        return carry
 
     def outputs(first):
         at = pl.ds(first, FINISH)
@@ -202,13 +201,14 @@
             )
         ]
 
-    def group(g, carry):
-        first = pl.multiple_of(g * FINISH, FINISH)
-        lax.fori_loop(0, FINISH, lambda i, c: step(first + i, c), 0, unroll=UNROLL)
-        at = pl.ds(first, FINISH)
+    for g in range(feats // FINISH):
+        first = g * FINISH
+        for f in range(first, first + FINISH):
+            step(f)
+        at = slice(first, first + FINISH)
         for half in range(2):
             lanes = slice(half * (BINS // 2), (half + 1) * (BINS // 2))
-            value = [halves[half][pl.ds(c * feats + first, FINISH), :] for c in range(cols)]
+            value = [halves[half][c * feats + first : c * feats + first + FINISH, :] for c in range(cols)]
             for c in range(cols):
                 leaf_ref[c, at, lanes] = value[c]
             pairs = [value[c] + value[c + 3] for c in (0, 1, 2, 6, 7, 8)]
@@ -218,9 +218,6 @@
                 node_ref[c, at, lanes] = pairs[c] + pairs[c + 3]
         for copy in outputs(first):
             copy.start()
-        return carry
-
-    lax.fori_loop(0, feats // FINISH, group, 0)
     for g in range(feats // FINISH):
         for copy in outputs(g * FINISH):
             copy.wait()
@@ -310,11 +307,11 @@
     )(got)
     rest = swap(half, 3)
     digit = jax.ShapeDtypeStruct((owners * feats, cap), F32)
-    hi, lo = pl.pallas_call(
+    hi, lo, moments = pl.pallas_call(
         prepare_kernel,
-        out_shape=[digit, digit],
+        out_shape=[digit, digit, jax.ShapeDtypeStruct((HI * 12, owners * cap), BF)],
         in_specs=specs(pltpu.VMEM, 1),
-        out_specs=specs(pltpu.VMEM, 2),
+        out_specs=specs(pltpu.VMEM, 3),
         compiler_params=params,
         name="prepare",
     )(got)
@@ -334,7 +331,7 @@
         ],
         compiler_params=params,
         name="hist",
-    )(got, hi, lo, half, rest)
+    )(hi, lo, moments, half, rest)
     return (
         node_moments.reshape(1, 3, feats, BINS),
         child_moments.reshape(2, 3, feats, BINS),

time: 43.3 us -> 43.2 us (level)
  no operation moved by 1% of the time
where the time goes in v6:
time: 43.2 us; the launch traced here: 42.9 us
  blocking collectives  21 us (49%)
  Pallas kernels  14.7 us (34%)
  starting transfers between devices  5.15 us (12%)
  waiting for transfers between devices  1.29 us (3%)
  between operations  0.84 us (2%)
    all_to_all x1, blocking collectives, on_device(): got = lax.all_to_all(buf, 'rows', 0, 0, tiled=True)  21 us
    pallas_call x1, Pallas kernels, on_device(): pl.pallas_call(hist_kernel, out_shape=[jax.ShapeDtypeStruct((n * 3, feats...  10.1 us
    ppermute x2, starting transfers between devices, on_device(): lax.ppermute(x, 'feat', [(i, i ^ bit) for i in range(feat_devices)])  5.15 us
    pallas_call x1, Pallas kernels, on_device(): pl.pallas_call(place_kernel, out_shape=[jax.ShapeDtypeStruct((nodes, dept...  2.37 us
    pallas_call x1, Pallas kernels, on_device(): pl.pallas_call(decide_kernel, out_shape=[jax.ShapeDtypeStruct((8, rows),...  1.43 us
    ppermute x2, waiting for transfers between devices, on_device(): lax.ppermute(x, 'feat', [(i, i ^ bit) for i in range(feat_devices)])  1.29 us
  transfers between devices with their start and end apart: 2, of which 1 were waited for; matrix products, arithmetic and copies ran while one was open for 0% of the time, Pallas kernels for 6%

profile of v6, /device:TPU:1, one launch (start us, length us, event | category | flops | bytes accessed | tf_op | source)
XLA Modules:
  0.0 42.9 jit_solution(15879668285047266374)
XLA Ops:
  0.6 1.4 %decide.1 = (bf16[8,2048]{1,0:T(8,128)(2,1)S(1)}, bf16[64,2048]{1,0:T(8,128)(2,1)S(1)}) custom-call(s32[1]{0:T(128)} %bitcast.place_ref, s32[1,2048]{1,0:T(1,128)} %bitcast.14, s32[64,2048]{1,0:T(8,128)} %bitcast.13, s32[1,32]{1,0:T(1,128)} %bitcast.19, s32[1,32]{1,0:T(1,128)} %bitcast.20, s32[1,64]{1,0:T(1,128)} %bitcast.21, s32[1,64]{1,0:T(1,128)} %bitcast.22), custom_call_target="tpu_custom_call" | custom-call | tf_op jit(solution)/shard_map/decide/pallas_call | solution.py:252
  2.1 2.2 %collective-permute-start = (bf16[8,2048]{1,0:T(8,128)(2,1)S(1)}, bf16[8,2048]{1,0:T(8,128)(2,1)S(1)}, u32[]{:S(2)}, u32[]{:S(2)}) collective-permute-start(bf16[8,2048]{1,0:T(8,128)(2,1)S(1)} %get-tuple-element.13.bits_ref), channel_id=1, source_target_pairs={{0,1},{1,0},{2,3},{3,2},{4,5},{5,4},{6,7},{7,6},{8,9},{9,8},{10,11... | collective-permute-start | bytes 98312 | tf_op jit(solution)/shard_map/ppermute | solution.py:250
  4.3 2.4 %place.1 = (bf16[32,72,128]{2,1,0:T(8,128)(2,1)S(1)}, f32[8,2048]{1,0:T(8,128)S(1)}) custom-call(bf16[64,2048]{1,0:T(8,128)(2,1)S(1)} %get-tuple-element.14.bins_ref, s32[1,2048]{1,0:T(1,128)} %bitcast.15, f32[1,2048]{1,0:T(1,128)} %bitcast.16, f32[1,2048]{1,0:T(1,128)} %bitcast.17, f32[1,2048]{1,0:T(1,128)} %bitcast.18), custom_call_target="tpu_custom_call" | custom-call | tf_op jit(solution)/shard_map/place/pallas_call | solution.py:273
  6.7 0.0 collective-permute-done.other_ref
  6.7 0.5 %value.1 = bf16[32,72,128]{2,1,0:T(8,128)(2,1)S(1)} custom-call(bf16[8,2048]{1,0:T(8,128)(2,1)S(1)} %get-tuple-element.13.bits_ref, bf16[8,2048]{1,0:T(8,128)(2,1)S(1)} %collective-permute-done.other_ref, f32[8,2048]{1,0:T(8,128)S(1)} %get-tuple-element.15.value_ref, bf16[32,72,128]{2,1,0:T(8,128)(2,1)S(1)} %get-tuple-element.16.buf_ref), custom_call_target="tpu_custom_call", output_to_operand_aliasing={{}: (3, {})} | custom-call | tf_op jit(solution)/shard_map/value/pallas_call | solution.py:289
  7.2 21.0 %all_to_all.5.got_ref = bf16[32,72,128]{2,1,0:T(8,128)(2,1)S(1)} all-to-all(bf16[32,72,128]{2,1,0:T(8,128)(2,1)S(1)} %value.1), channel_id=1, replica_groups=mesh['rows'=32,'feat'=4] {'rows'}, dimensions={0} | all-to-all | bytes 1179648 | tf_op jit(solution)/shard_map/all_to_all | solution.py:299
  28.2 2.9 %collective-permute-start.1 = (bf16[3,32,128]{2,1,0:T(8,128)(2,1)S(1)}, bf16[3,32,128]{2,1,0:T(8,128)(2,1)S(1)}, u32[]{:S(2)}, u32[]{:S(2)}) collective-permute-start(bf16[3,32,128]{2,1,0:T(8,128)(2,1)S(1)} %tail.1.bits_ref), channel_id=1, source_target_pairs={{0,3},{1,2},{2,1},{3,0},{4,7},{5,6},{6,5},{7,4},{8,11},{9,10},{10,... | collective-permute-start | bytes 73736 | tf_op jit(solution)/shard_map/ppermute | solution.py:250
  31.1 0.3 prepare.1
  31.4 1.3 %collective-permute-done.1.other_ref = bf16[3,32,128]{2,1,0:T(8,128)(2,1)S(1)} collective-permute-done((bf16[3,32,128]{2,1,0:T(8,128)(2,1)S(1)}, bf16[3,32,128]{2,1,0:T(8,128)(2,1)S(1)}, u32[]{:S(2)}, u32[]{:S(2)}) %collective-permute-start.1) | collective-permute-done | bytes 24608 | tf_op jit(solution)/shard_map/ppermute | solution.py:250
  32.7 10.1 %hist.1 = (f32[3,64,256]{2,1,0:T(8,128)}, f32[6,64,256]{2,1,0:T(8,128)}, f32[12,64,256]{2,1,0:T(8,128)}) custom-call(f32[2048,128]{1,0:T(8,128)S(1)} %get-tuple-element.17.hi_ref, f32[2048,128]{1,0:T(8,128)S(1)} %get-tuple-element.18.lo_ref, bf16[48,4096]{1,0:T(8,128)(2,1)S(1)} %get-tuple-element.19.moment_ref, bf16[3,32,128]{2,1,0:T(8,128)(2,1)S(1)} %tail.1.bits_ref, ...), custom_call_target="tpu_custom_call" | custom-call | tf_op jit(solution)/shard_map/hist/pallas_call | solution.py:318
  (1 shorter events, 0.0 us)
Async XLA Ops:
  2.1 4.6 %collective-permute-start = (bf16[8,2048]{1,0:T(8,128)(2,1)S(1)}, bf16[8,2048]{1,0:T(8,128)(2,1)S(1)}, u32[]{:S(2)}, u32[]{:S(2)}) collective-permute-start(bf16[8,2048]{1,0:T(8,128)(2,1)S(1)} %get-tuple-element.13.bits_ref), channel_id=1, source_target_pairs={{0,1},{1,0},{2,3},{3,2},{4,5},{5,4},{6,7},{7,6},{8,9},{9,8},{10,11... | collective-permute-start | bytes 98312 | tf_op jit(solution)/shard_map/ppermute | solution.py:250
  28.2 4.5 %collective-permute-start.1 = (bf16[3,32,128]{2,1,0:T(8,128)(2,1)S(1)}, bf16[3,32,128]{2,1,0:T(8,128)(2,1)S(1)}, u32[]{:S(2)}, u32[]{:S(2)}) collective-permute-start(bf16[3,32,128]{2,1,0:T(8,128)(2,1)S(1)} %tail.1.bits_ref), channel_id=1, source_target_pairs={{0,3},{1,2},{2,1},{3,0},{4,7},{5,6},{6,5},{7,4},{8,11},{9,10},{10,... | collective-permute-start | bytes 73736 | tf_op jit(solution)/shard_map/ppermute | solution.py:250

commit v7 on v6

--- a/solution.py
+++ b/solution.py
@@ -65,14 +65,13 @@
 
 
 def place_kernel(
-    bins_ref, node_hbm, w_hbm, t_hbm, y_hbm, out_ref, value_ref, node_ref, w_ref, t_ref, y_ref, a_ref,
+    bins_ref, node_ref, w_hbm, t_hbm, y_hbm, out_ref, value_ref, hot_ref, w_ref, t_ref, y_ref, a_ref,
     sems,
 ):
-    copies = start_all(((node_hbm, node_ref), (w_hbm, w_ref), (t_hbm, t_ref), (y_hbm, y_ref)), sems)
+    copies = start_all(((w_hbm, w_ref), (t_hbm, t_ref), (y_hbm, y_ref)), sems)
     feats, rows = bins_ref.shape
     nodes, depth, cap = out_ref.shape
     blocks = rows // 256
-    copies[0].wait()
     node = node_ref[...]
     hot = (iota((nodes, rows), 0) == node).astype(F32)
     stacked = jnp.concatenate([hot[:, b * 256 : (b + 1) * 256] for b in range(blocks)], 0)
@@ -89,6 +88,7 @@
     rank = jnp.concatenate(ranks, 1)
     code = rank.astype(jnp.int32) + node % 2 * cap
     slot_hot = (iota((2 * cap, rows), 0) == code).astype(F32).astype(BF)
+    hot_ref[...] = slot_hot
     bins = bins_ref[...]
     pair = jnp.broadcast_to(node // 2, (feats, rows))
     for p in range(nodes // 2):
@@ -98,28 +98,26 @@
         piece = moved[p * feats : (p + 1) * feats]
         out_ref[2 * p, :feats, :] = piece[:, :cap]
         out_ref[2 * p + 1, :feats, :] = piece[:, cap:]
-    for copy in copies[1:]:
+    for copy in copies:
         copy.wait()
     w = w_ref[...]
     t = t_ref[...]
     y = y_ref[...]
     value_ref[...] = jnp.concatenate(
-        [w, w * t * t, w * t * y, code.astype(F32), (node // 2).astype(F32), jnp.zeros((3, rows), F32)], 0
-    )
-
-
-def value_kernel(bits_ref, other_ref, value_ref, buf_ref, out_ref, part_ref, sem):
+        [w, w * t * t, w * t * y, (node // 2).astype(F32), jnp.zeros((4, rows), F32)], 0
+    )
+
+
+def value_kernel(bits_ref, other_ref, value_ref, hot_ref, buf_ref, out_ref, part_ref, sem):
     nodes, _, cap = part_ref.shape
     rows = value_ref.shape[1]
     bits = bits_ref[...].astype(F32) + other_ref[...].astype(F32)
     carried = jnp.concatenate([value_ref[:3, :], bits[:5]], 0)
-    code = value_ref[3:4, :].astype(jnp.int32)
-    slot_hot = (iota((2 * cap, rows), 0) == code).astype(F32).astype(BF)
-    pair = jnp.broadcast_to(value_ref[4:5, :], (8, rows))
+    pair = jnp.broadcast_to(value_ref[3:4, :], (8, rows))
     spread = jnp.concatenate(
         [jnp.where(pair == float(p), carried, 0.0) for p in range(nodes // 2)], 0
     ).astype(BF)
-    moved = lax.dot_general(spread, slot_hot, NT, preferred_element_type=F32).astype(BF)
+    moved = lax.dot_general(spread, hot_ref[...], NT, preferred_element_type=F32).astype(BF)
     for p in range(nodes // 2):
         piece = moved[p * 8 : (p + 1) * 8]
         part_ref[2 * p] = piece[:, :cap]
@@ -249,13 +247,16 @@
     row = lambda dtype: pltpu.VMEM((1, rows), dtype)
     swap = lambda x, bit: lax.ppermute(x, "feat", [(i, i ^ bit) for i in range(feat_devices)])
     bins, node = in_hbm(binned.T, node_index.T)
-    own, narrow = pl.pallas_call(
+    own, narrow, kept = pl.pallas_call(
         decide_kernel,
-        out_shape=[jax.ShapeDtypeStruct((8, rows), BF), jax.ShapeDtypeStruct((feats, rows), BF)],
+        out_shape=[
+            jax.ShapeDtypeStruct((8, rows), BF),
+            jax.ShapeDtypeStruct((feats, rows), BF),
+            jax.ShapeDtypeStruct((1, rows), jnp.int32),
+        ],
         in_specs=specs(pltpu.SMEM, 1) + specs(pltpu.HBM, 6),
-        out_specs=specs(pltpu.VMEM, 2),
+        out_specs=specs(pltpu.VMEM, 3),
         scratch_shapes=[
-            row(jnp.int32),
             pltpu.VMEM((feats, rows), jnp.int32),
             pltpu.VMEM((1, nodes), jnp.int32),
             pltpu.VMEM((1, nodes), jnp.int32),
@@ -269,33 +270,34 @@
         lax.axis_index("feat").astype(jnp.int32)[None], node, bins,
         *in_hbm(root_feature[None], root_cutoff[None], child_feature[None], child_cutoff[None]),
     )
-    other = swap(own, 1)
-    buf, value = pl.pallas_call(
+    other = swap(own, 2)
+    buf, value, slot_hot = pl.pallas_call(
         place_kernel,
         out_shape=[
             jax.ShapeDtypeStruct((nodes, depth, cap), BF),
             jax.ShapeDtypeStruct((8, rows), F32),
-        ],
-        in_specs=specs(pltpu.VMEM, 1) + specs(pltpu.HBM, 4),
-        out_specs=specs(pltpu.VMEM, 2),
+            jax.ShapeDtypeStruct((2 * cap, rows), BF),
+        ],
+        in_specs=specs(pltpu.VMEM, 2) + specs(pltpu.HBM, 3),
+        out_specs=specs(pltpu.VMEM, 3),
         scratch_shapes=[
-            row(jnp.int32), row(F32), row(F32), row(F32),
+            row(F32), row(F32), row(F32),
             pltpu.VMEM((nodes // 2 * feats, rows), BF),
-            pltpu.SemaphoreType.DMA((4,)),
+            pltpu.SemaphoreType.DMA((3,)),
         ],
         compiler_params=params,
         name="place",
-    )(narrow, node, *in_hbm(unit_weight[None], treatment[None], outcome[None]))
+    )(narrow, kept, *in_hbm(unit_weight[None], treatment[None], outcome[None]))
     buf = pl.pallas_call(
         value_kernel,
         out_shape=jax.ShapeDtypeStruct((nodes, depth, cap), BF),
-        in_specs=specs(pltpu.VMEM, 3) + specs(pl.ANY, 1),
+        in_specs=specs(pltpu.VMEM, 4) + specs(pl.ANY, 1),
         out_specs=specs(pl.ANY, 1)[0],
         scratch_shapes=[pltpu.VMEM((nodes, 8, cap), BF), pltpu.SemaphoreType.DMA],
-        input_output_aliases={3: 0},
+        input_output_aliases={4: 0},
         compiler_params=params,
         name="value",
-    )(own, other, value, buf)
+    )(own, other, value, slot_hot, buf)
     got = lax.all_to_all(buf, "rows", 0, 0, tiled=True)
     half = pl.pallas_call(
         tail_kernel,
@@ -305,7 +307,7 @@
         compiler_params=params,
         name="tail",
     )(got)
-    rest = swap(half, 3)
+    rest = swap(half, 1)
     digit = jax.ShapeDtypeStruct((owners * feats, cap), F32)
     hi, lo, moments = pl.pallas_call(
         prepare_kernel,

time: 43.2 us -> 43.3 us (level)
  Pallas kernels: 14.7 us -> 14.1 us
    pallas_call x1, Pallas kernels: 2.37 us -> 1.81 us  [on_device(): pl.pallas_call(place_kernel, out_shape=[jax.ShapeDtypeStruct((nodes, dept...]
  transfers between devices with their start and end apart: 2 -> 2, of which waited for: 1 -> 1; matrix products, arithmetic and copies ran while one was open for 0% -> 0% of each run, Pallas kernels for 6% -> 5%
where the time goes in v7:
time: 43.3 us; the launch traced here: 43.1 us
  blocking collectives  21.4 us (49%)
  Pallas kernels  14.1 us (33%)
  starting transfers between devices  5.38 us (12%)
  waiting for transfers between devices  1.43 us (3%)
  between operations  0.84 us (2%)
    all_to_all x1, blocking collectives, on_device(): got = lax.all_to_all(buf, 'rows', 0, 0, tiled=True)  21.4 us
    pallas_call x1, Pallas kernels, on_device(): pl.pallas_call(hist_kernel, out_shape=[jax.ShapeDtypeStruct((n * 3, feats...  10.1 us
    ppermute x2, starting transfers between devices, on_device(): lax.ppermute(x, 'feat', [(i, i ^ bit) for i in range(feat_devices)])  5.38 us
    pallas_call x1, Pallas kernels, on_device(): pl.pallas_call(place_kernel, out_shape=[jax.ShapeDtypeStruct((nodes, dept...  1.81 us
    ppermute x2, waiting for transfers between devices, on_device(): lax.ppermute(x, 'feat', [(i, i ^ bit) for i in range(feat_devices)])  1.43 us
    pallas_call x1, Pallas kernels, on_device(): pl.pallas_call(decide_kernel, out_shape=[jax.ShapeDtypeStruct((8, rows),...  1.43 us
  transfers between devices with their start and end apart: 2, of which 1 were waited for; matrix products, arithmetic and copies ran while one was open for 0% of the time, Pallas kernels for 5%

profile of v7, /device:TPU:1, one launch (start us, length us, event | category | flops | bytes accessed | tf_op | source)
XLA Modules:
  0.0 43.1 jit_solution(1414073223970406276)
XLA Ops:
  0.6 1.4 %decide.1 = (bf16[8,2048]{1,0:T(8,128)(2,1)S(1)}, bf16[64,2048]{1,0:T(8,128)(2,1)S(1)}, s32[1,2048]{1,0:T(1,128)S(1)}) custom-call(s32[1]{0:T(128)} %bitcast.place_ref, s32[1,2048]{1,0:T(1,128)} %bitcast.14, s32[64,2048]{1,0:T(8,128)} %bitcast.13, s32[1,32]{1,0:T(1,128)} %bitcast.18, s32[1,32]{1,0:T(1,128)} %bitcast.19, s32[1,64]{1,0:T(1,128)} %bitcast.20, ...), custom_call_target="tpu_custom_call" | custom-call | tf_op jit(solution)/shard_map/decide/pallas_call | solution.py:250
  2.1 3.8 %collective-permute-start = (bf16[8,2048]{1,0:T(8,128)(2,1)S(1)}, bf16[8,2048]{1,0:T(8,128)(2,1)S(1)}, u32[]{:S(2)}, u32[]{:S(2)}) collective-permute-start(bf16[8,2048]{1,0:T(8,128)(2,1)S(1)} %get-tuple-element.15.bits_ref), channel_id=1, source_target_pairs={{0,2},{1,3},{2,0},{3,1},{4,6},{5,7},{6,4},{7,5},{8,10},{9,11},{10,... | collective-permute-start | bytes 98312 | tf_op jit(solution)/shard_map/ppermute | solution.py:248
  5.9 1.8 %place.1 = (bf16[32,72,128]{2,1,0:T(8,128)(2,1)S(1)}, f32[8,2048]{1,0:T(8,128)S(1)}, bf16[256,2048]{1,0:T(8,128)(2,1)S(1)}) custom-call(bf16[64,2048]{1,0:T(8,128)(2,1)S(1)} %get-tuple-element.16.bins_ref, s32[1,2048]{1,0:T(1,128)S(1)} %get-tuple-element.17.node_ref, f32[1,2048]{1,0:T(1,128)} %bitcast.15, f32[1,2048]{1,0:T(1,128)} %bitcast.16, ...), custom_call_target="tpu_custom_call" | custom-call | tf_op jit(solution)/shard_map/place/pallas_call | solution.py:274
  7.7 0.0 collective-permute-done.other_ref
  7.7 0.5 %value.1 = bf16[32,72,128]{2,1,0:T(8,128)(2,1)S(1)} custom-call(bf16[8,2048]{1,0:T(8,128)(2,1)S(1)} %get-tuple-element.15.bits_ref, bf16[8,2048]{1,0:T(8,128)(2,1)S(1)} %collective-permute-done.other_ref, f32[8,2048]{1,0:T(8,128)S(1)} %get-tuple-element.18.value_ref, ...), custom_call_target="tpu_custom_call", output_to_operand_aliasing={{}: (4, {})} | custom-call | tf_op jit(solution)/shard_map/value/pallas_call | solution.py:291
  8.2 21.4 %all_to_all.5.got_ref = bf16[32,72,128]{2,1,0:T(8,128)(2,1)S(1)} all-to-all(bf16[32,72,128]{2,1,0:T(8,128)(2,1)S(1)} %value.1), channel_id=1, replica_groups=mesh['rows'=32,'feat'=4] {'rows'}, dimensions={0} | all-to-all | bytes 1179648 | tf_op jit(solution)/shard_map/all_to_all | solution.py:301
  29.6 1.6 %collective-permute-start.1 = (bf16[3,32,128]{2,1,0:T(8,128)(2,1)S(1)}, bf16[3,32,128]{2,1,0:T(8,128)(2,1)S(1)}, u32[]{:S(2)}, u32[]{:S(2)}) collective-permute-start(bf16[3,32,128]{2,1,0:T(8,128)(2,1)S(1)} %tail.1.bits_ref), channel_id=1, source_target_pairs={{0,1},{1,0},{2,3},{3,2},{4,5},{5,4},{6,7},{7,6},{8,9},{9,8},{10,11... | collective-permute-start | bytes 73736 | tf_op jit(solution)/shard_map/ppermute | solution.py:248
  31.2 0.3 prepare.1
  31.5 1.4 %collective-permute-done.1.other_ref = bf16[3,32,128]{2,1,0:T(8,128)(2,1)S(1)} collective-permute-done((bf16[3,32,128]{2,1,0:T(8,128)(2,1)S(1)}, bf16[3,32,128]{2,1,0:T(8,128)(2,1)S(1)}, u32[]{:S(2)}, u32[]{:S(2)}) %collective-permute-start.1) | collective-permute-done | bytes 24608 | tf_op jit(solution)/shard_map/ppermute | solution.py:248
  32.9 10.1 %hist.1 = (f32[3,64,256]{2,1,0:T(8,128)}, f32[6,64,256]{2,1,0:T(8,128)}, f32[12,64,256]{2,1,0:T(8,128)}) custom-call(f32[2048,128]{1,0:T(8,128)S(1)} %get-tuple-element.21.hi_ref, f32[2048,128]{1,0:T(8,128)S(1)} %get-tuple-element.22.lo_ref, bf16[48,4096]{1,0:T(8,128)(2,1)S(1)} %get-tuple-element.23.moment_ref, bf16[3,32,128]{2,1,0:T(8,128)(2,1)S(1)} %tail.1.bits_ref, ...), custom_call_target="tpu_custom_call" | custom-call | tf_op jit(solution)/shard_map/hist/pallas_call | solution.py:320
  (1 shorter events, 0.0 us)
Async XLA Ops:
  2.1 5.6 %collective-permute-start = (bf16[8,2048]{1,0:T(8,128)(2,1)S(1)}, bf16[8,2048]{1,0:T(8,128)(2,1)S(1)}, u32[]{:S(2)}, u32[]{:S(2)}) collective-permute-start(bf16[8,2048]{1,0:T(8,128)(2,1)S(1)} %get-tuple-element.15.bits_ref), channel_id=1, source_target_pairs={{0,2},{1,3},{2,0},{3,1},{4,6},{5,7},{6,4},{7,5},{8,10},{9,11},{10,... | collective-permute-start | bytes 98312 | tf_op jit(solution)/shard_map/ppermute | solution.py:248
  29.6 3.3 %collective-permute-start.1 = (bf16[3,32,128]{2,1,0:T(8,128)(2,1)S(1)}, bf16[3,32,128]{2,1,0:T(8,128)(2,1)S(1)}, u32[]{:S(2)}, u32[]{:S(2)}) collective-permute-start(bf16[3,32,128]{2,1,0:T(8,128)(2,1)S(1)} %tail.1.bits_ref), channel_id=1, source_target_pairs={{0,1},{1,0},{2,3},{3,2},{4,5},{5,4},{6,7},{7,6},{8,9},{9,8},{10,11... | collective-permute-start | bytes 73736 | tf_op jit(solution)/shard_map/ppermute | solution.py:248
